TPU v7x, 256 devices: a whole 4x4x8 slice. The times are simulated.
256 devices in a mesh: section: 4 (over x), ex: 16 (over z, core), tp: 4 (over y).
Axes of the slice: x: 4, y: 4, z: 8, core: 2. Of those that a mesh axis runs over, the one named last changes fastest.
Arguments:
- clean_heads: bfloat16 [4, 16, 512, 4096], P('section', 'ex', None, 'tp'), may hold values from -6 to 6
- corrupt_heads: bfloat16 [4, 16, 512, 4096], P('section', 'ex', None, 'tp'), may hold values from -6 to 6
- donors: int32 [512, 16], P('ex'), may hold values from 0 to 15, each once within a row
- senders: int32 [4, 8], P('section', 'tp'), may hold values from 0 to 31, as said below
- out_weight: bfloat16 [4, 4096, 8192], P('section', 'tp', 'ex'), may hold values from -0.1875 to 0.1875
- residual: bfloat16 [4, 16, 512, 8192], P('section', 'ex', None, 'tp'), may hold values from -160 to 160
- norm_gain: bfloat16 [4, 8192], P('section', 'tp'), may hold values from 0.25 to 1.75
- value_weight: bfloat16 [4, 8192, 1024], P('section', 'tp', 'ex'), may hold values from -0.0625 to 0.0625
- clean_values: bfloat16 [4, 16, 512, 1024], P('section', 'ex', None, 'tp'), may hold values from -6 to 6
- queries: bfloat16 [4, 16, 512, 4096], P('section', 'ex', None, 'tp'), may hold values from -120 to 120
- key_vectors: bfloat16 [4, 16, 512, 1024], P('section', 'ex', None, 'tp'), may hold values from -4 to 4
- receivers: int32 [4, 32], P('section', 'tp'), may hold values 0 or 1
Outputs:
- attended: bfloat16 [4, 16, 512, 4096], P('section', 'ex', None, 'tp')
Inputs may be any that keep to these rules, and one draw needn't show every extreme that they name: `donors`: each position's row is a permutation of the 16 examples. `senders`: in each section's row, entries j * 2 to (j + 1) * 2 - 1 are distinct heads of j * 8 to (j + 1) * 8 - 1.
All inputs are finite; a program needn't handle non-finite values. No bound on the sum of `receivers` on one device may be relied on, other than what follows from the above.
Results may differ from a plain program's by a relative error of at most 0.012.
Values may be sent and summed in bfloat16 or wider, within the bound.
A program may use at most 128 MiB of HBM per device.

v0:
```python
import math

import jax
import jax.numpy as jnp
from jax import lax
from jax.sharding import PartitionSpec as P

D = 8192
HD = 128
GROUP = 4


def sent_to_all(array, axis):
    copies = jnp.broadcast_to(array, (lax.axis_size(axis), *array.shape))
    return lax.all_to_all(copies, axis, split_axis=0, concat_axis=0, tiled=True)


def of_everyone(array, axis):
    everything = sent_to_all(array, axis)
    return jnp.sum(everything, axis=0)


def cut_along(array, dim, peers):
    before, after = (array.shape[:dim], array.shape[dim + 1 :])
    return jnp.moveaxis(array.reshape(*before, peers, -1, *after), dim, 0)


def sent_and_summed(array, axis, dim):
    peers = lax.axis_size(axis)
    pieces = lax.all_to_all(cut_along(array, dim, peers), axis, 0, 0, tiled=True)
    return jnp.sum(pieces.astype(jnp.float32), axis=0)


def attend(queries, key_vectors, chosen):
    scores = jnp.einsum(
        "etkgd,eukd->ekgtu", queries, key_vectors, preferred_element_type=jnp.float32
    )
    scores = scores * (1.0 / math.sqrt(HD))
    places = jnp.arange(scores.shape[-1])
    causal = places[:, None] >= places[None, :]
    scores = jnp.where(causal, scores, -jnp.inf)
    maxima = jnp.max(scores, axis=-1, keepdims=True)
    exponent = jnp.exp(scores - maxima)
    weights = (exponent / jnp.sum(exponent, axis=-1, keepdims=True)).astype(jnp.bfloat16)
    return jnp.einsum("ekgtu,eukgd->etkgd", weights, chosen, preferred_element_type=jnp.float32)


def per_device(
    clean_heads,
    corrupt_heads,
    donors,
    senders,
    out_weight,
    residual,
    norm_gain,
    value_weight,
    clean_values,
    queries,
    key_vectors,
    receivers,
):
    examples, length = (residual.shape[1], residual.shape[2])
    row_count = examples * length
    heads_here = clean_heads.shape[3] // HD
    local_ids = senders[0] - lax.axis_index("tp") * heads_here
    weight_rows = out_weight[0]
    corrupt = jnp.take(
        corrupt_heads[0].reshape(examples, length, heads_here, HD), local_ids, axis=2
    ).reshape(examples, length, -1)
    clean_part = jnp.take(
        clean_heads[0].reshape(examples, length, heads_here, HD), local_ids, axis=2
    ).reshape(examples, length, -1)
    weight_rows = jnp.take(weight_rows.reshape(heads_here, HD, -1), local_ids, axis=0).reshape(
        local_ids.shape[0] * HD, -1
    )
    sender_mask = jnp.ones((local_ids.shape[0],), jnp.bool_)
    gathered = lax.all_to_all(corrupt, "ex", split_axis=1, concat_axis=0, tiled=True)
    everyone = gathered.shape[0]
    onehot = (donors[:, :, None] == jnp.arange(everyone)[None, None, :]).astype(jnp.bfloat16)
    patched = jnp.einsum(
        "tef,ftc->etc", onehot, gathered, preferred_element_type=jnp.float32
    ).astype(jnp.bfloat16)
    returned = lax.all_to_all(patched, "ex", split_axis=0, concat_axis=1, tiled=True)
    chosen_count = returned.shape[-1] // HD
    difference = returned.astype(jnp.float32) - clean_part.astype(jnp.float32)
    difference = jnp.where(
        sender_mask[None, None, :, None],
        difference.reshape(examples, length, chosen_count, HD),
        0.0,
    )
    difference = difference.astype(jnp.bfloat16).reshape(row_count, chosen_count * HD)
    partials = jnp.dot(
        difference,
        lax.all_gather(weight_rows, "ex", axis=1, tiled=True),
        preferred_element_type=jnp.float32,
    )
    increment = lax.psum_scatter(
        partials.astype(jnp.bfloat16), "tp", scatter_dimension=1, tiled=True
    ).astype(jnp.float32)
    every_section = lax.all_gather(
        increment[None].astype(jnp.bfloat16), "section", axis=0, tiled=True
    ).astype(jnp.float32)
    earlier_mask = (jnp.arange(every_section.shape[0]) <= lax.axis_index("section")).astype(
        jnp.float32
    )
    carried = jnp.sum(every_section * earlier_mask[:, None, None], axis=0)
    stream = residual[0].reshape(row_count, -1).astype(jnp.float32) + carried
    squares = of_everyone(jnp.sum(stream * stream, axis=-1), "tp")
    normed = (
        stream * lax.rsqrt(squares[:, None] / D + 1e-05) * norm_gain[0].astype(jnp.float32)
    ).astype(jnp.bfloat16)
    value_terms = jnp.dot(
        normed,
        lax.all_gather(value_weight[0], "ex", axis=1, tiled=True),
        preferred_element_type=jnp.float32,
    )
    values = sent_and_summed(value_terms.astype(jnp.bfloat16), "tp", 1).astype(jnp.bfloat16)
    kv_here = values.shape[-1] // HD
    values = values.reshape(examples, length, kv_here, 1, HD)
    clean_here = clean_values[0].reshape(examples, length, kv_here, 1, HD)
    receive_flags = receivers[0].reshape(kv_here, GROUP)
    chosen = jnp.where((receive_flags == 1)[None, None, :, :, None], values, clean_here)
    attended = attend(
        queries[0].reshape(examples, length, kv_here, GROUP, HD),
        key_vectors[0].reshape(examples, length, kv_here, HD),
        chosen,
    )
    return attended.reshape(1, examples, length, -1).astype(jnp.bfloat16)


def solution(mesh):
    return jax.shard_map(
        per_device,
        mesh=mesh,
        in_specs=(
            P("section", "ex", None, "tp"),
            P("section", "ex", None, "tp"),
            P("ex", None),
            P("section", "tp"),
            P("section", "tp", "ex"),
            P("section", "ex", None, "tp"),
            P("section", "tp"),
            P("section", "tp", "ex"),
            P("section", "ex", None, "tp"),
            P("section", "ex", None, "tp"),
            P("section", "ex", None, "tp"),
            P("section", "tp"),
        ),
        out_specs=P("section", "ex", None, "tp"),
        check_vma=False,
    )
```

profile of v0, /device:TPU:7, one launch (start us, length us, event | category | flops | bytes accessed | tf_op | source)
XLA Modules:
  0.0 325.8 jit_solution(17450604061688993394)
XLA Ops:
  6.5 0.8 compare_and_fusion
  7.3 0.7 fusion.28
  8.0 0.6 gather_fusion
  8.6 0.8 bitcast_select_fusion.3
  9.4 1.5 copy.82
  10.9 0.7 copy.83
  11.6 0.6 gather_fusion.1
  12.3 0.1 copy.84
  12.5 0.4 copy.85
  12.9 0.5 broadcast.165
  13.4 2.2 reduce.8
  15.7 0.8 reshape.224
  16.4 9.2 %all-to-all-start = ((bf16[16,2,4096]{2,1,0:T(2,128)(2,1)}), bf16[16,2,4096]{2,1,0:T(2,128)(2,1)S(1)}, u32[]{:S(2)}, u32[]{:S(2)}) async-start(bf16[16,2,4096]{2,1,0:T(2,128)(2,1)} %reshape.224), calls=%async_computation | async-start | bytes 524288 | tf_op jit(solution)/shard_map/all_to_all | solution.py:77
  25.7 14.4 %all-to-all-done = bf16[16,2,4096]{2,1,0:T(2,128)(2,1)S(1)} async-done(((bf16[16,2,4096]{2,1,0:T(2,128)(2,1)}), bf16[16,2,4096]{2,1,0:T(2,128)(2,1)S(1)}, u32[]{:S(2)}, u32[]{:S(2)}) %all-to-all-start) | async-done | bytes 262176 | tf_op jit(solution)/shard_map/all_to_all | solution.py:77
  40.1 0.3 reshape.225
  40.4 0.3 fusion.17
  40.7 0.8 copy.88
  41.5 3.4 %all-to-all-start.1 = ((bf16[16,32,256]{2,1,0:T(8,128)(2,1)}), bf16[16,32,256]{2,1,0:T(8,128)(2,1)S(1)}, u32[]{:S(2)}, u32[]{:S(2)}) async-start(bf16[16,32,256]{2,1,0:T(8,128)(2,1)} %copy.88), calls=%async_computation.1 | async-start | bytes 524288 | tf_op jit(solution)/shard_map/all_to_all | solution.py:83
  45.0 0.5 copy.89
  45.6 0.7 copy.90
  46.3 0.6 gather_fusion.2
  46.9 12.3 %all-to-all-done.1 = bf16[16,32,256]{2,1,0:T(8,128)(2,1)S(1)} async-done(((bf16[16,32,256]{2,1,0:T(8,128)(2,1)}), bf16[16,32,256]{2,1,0:T(8,128)(2,1)S(1)}, u32[]{:S(2)}, u32[]{:S(2)}) %all-to-all-start.1) | async-done | bytes 262176 | tf_op jit(solution)/shard_map/all_to_all | solution.py:83
  59.2 0.3 reshape.173
  59.5 0.1 fusion.22
  59.6 0.1 copy.92
  59.8 4.0 %all-gather.6.cloned.1.call-done = bf16[256,8192]{1,0:T(8,128)(2,1)} async-done(((bf16[256,512]{1,0:T(8,128)(2,1)}), bf16[256,8192]{1,0:T(8,128)(2,1)}) %all-gather.6.cloned.1.call-update) | async-done | bytes 4194320 | tf_op jit(solution)/shard_map/all_gather | solution.py:94
  63.8 7.8 %convolution_convert_fusion = bf16[512,8192]{1,0:T(8,128)(2,1)} fusion(bf16[512,256]{0,1:T(8,128)(2,1)S(1)} %bitcast.99, bf16[256,8192]{1,0:T(8,128)(2,1)} %all-gather.6.cloned.1.call-done), kind=kOutput, calls=%fused_computation.5 | convolution fusion | flops 2151677952 | bytes 12845056 | tf_op jit(solution)/shard_map/dot_general | solution.py:92
  71.6 81.9 %reduce-scatter.2.cloned.1.call-done = bf16[512,2048]{1,0:T(8,128)(2,1)} async-done(((bf16[512,8192]{1,0:T(8,128)(2,1)}), bf16[512,2048]{1,0:T(8,128)(2,1)}) %reduce-scatter.2.cloned.1.call-update) | async-done | bytes 2097168 | tf_op jit(solution)/shard_map/reduce_scatter | solution.py:97
  153.6 0.5 all-gather.10.cloned.1.call-update
  154.1 84.8 %all-gather.8.cloned.1.call-done = bf16[2048,2048]{1,0:T(8,128)(2,1)} async-done(((bf16[512,2048]{1,0:T(8,128)(2,1)}), bf16[2048,2048]{1,0:T(8,128)(2,1)}) %all-gather.8.cloned.1.call-update) | async-done | bytes 8388624 | tf_op jit(solution)/shard_map/all_gather | solution.py:100
  239.0 6.1 %fusion = f32[512,2048]{1,0:T(8,128)S(1)} fusion(bf16[4,512,2048]{2,1,0:T(8,128)(2,1)} %bitcast.92, f32[4]{0:T(128)S(1)} %compare_convert_fusion), kind=kLoop, calls=%fused_computation.4 | loop fusion | flops 11534336 | bytes 12582928 | tf_op jit(solution)/shard_map/reduce_sum | solution.py:106
  245.2 1.9 copy-done.1
  247.1 0.6 multiply_reduce_fusion
  247.7 0.6 broadcast_in_dim.86
  248.3 4.8 %all-to-all-start.2 = ((f32[4,1,512]{2,1,0:T(1,128)}), f32[4,1,512]{2,1,0:T(1,128)S(1)}, u32[]{:S(2)}, u32[]{:S(2)}) async-start(f32[4,1,512]{2,1,0:T(1,128)} %broadcast_in_dim.86), calls=%async_computation.3 | async-start | bytes 16384 | tf_op jit(solution)/shard_map/all_to_all | solution.py:15
  253.2 2.6 reshape.170
  255.8 1.7 reshape.169
  257.6 28.4 %all-gather.10.cloned.1.call-done = bf16[1,2048,1024]{1,2,0:T(8,128)(2,1)} async-done(((bf16[1,2048,64]{1,2,0:T(8,128)(2,1)}), bf16[1,2048,1024]{1,2,0:T(8,128)(2,1)}) %all-gather.10.cloned.1.call-update) | async-done | bytes 4194320 | tf_op jit(solution)/shard_map/all_gather | solution.py:114
  286.0 5.8 %fusion.11 = bf16[512,1024]{1,0:T(8,128)(2,1)S(1)} fusion(bf16[1,2048,1024]{1,2,0:T(8,128)(2,1)} %all-gather.10.cloned.1.call-done, f32[512,2048]{1,0:T(8,128)} %copy-done.1, bf16[1,1,512,2048]{3,2,1,0:T(8,128)(2,1)S(1)} %copy-done.2, f32[2048]{0:T(1024)S(1)} %bitcast.107, f32[512]{0:T(512)S(1)} %add_rsqrt_fusion), kind=kOutput, calls=%fused_computation.22 | convolution fusion | flops 2153250816 | bytes 11544576 | tf_op jit(solution)/shard_map/dot_general | solution.py:112
  291.8 1.1 copy.126
  292.9 4.0 %all-to-all-start.3 = ((bf16[4,512,256]{2,1,0:T(8,128)(2,1)}), bf16[4,512,256]{2,1,0:T(8,128)(2,1)S(1)}, u32[]{:S(2)}, u32[]{:S(2)}) async-start(bf16[4,512,256]{2,1,0:T(8,128)(2,1)} %bitcast.90), calls=%async_computation.4 | async-start | bytes 2097152 | tf_op jit(solution)/shard_map/all_to_all | solution.py:30
  297.0 5.7 %fusion.2 = (f32[2,4,512]{2,1,0:T(4,128)S(1)}, f32[2,512,512,4]{2,1,3,0:T(8,128)}) fusion(pred[512,512]{0,1:T(8,128)(4,1)S(1)} %iota_compare_fusion, bf16[512,2,4,128]{3,2,1,0:T(4,128)(2,1)S(1)} %copy-done.4, bf16[512,2,128,1]{2,1,0,3:T(2,128)(2,1)} %bitcast.104), kind=kOutput, calls=%fused_computation.10 | convolution fusion | flops 543158272 | bytes 9977856 | tf_op jit(solution)/shard_map/etkgd,eukd->ekgtu/dot_general | solution.py:35
  302.7 1.1 copy.105
  303.9 5.1 %fusion.1 = f32[2,4,512]{2,1,0:T(4,128)S(1)} fusion(f32[2,512,512,4]{2,1,3,0:T(8,128)} %get-tuple-element.9, f32[2,4,512]{2,1,0:T(4,128)S(1)} %get-tuple-element.8, pred[512,512]{0,1:T(8,128)(4,1)S(1)} %iota_compare_fusion), kind=kLoop, calls=%fused_computation.9 | loop fusion | flops 8384512 | bytes 8683520 | tf_op jit(solution)/shard_map/reduce_sum | solution.py:44
  309.0 2.6 all-to-all-done.3
  311.6 0.3 reduce_sum.51
  312.0 5.9 %fusion.14 = bf16[2,4,128,512]{3,2,1,0:T(8,128)(2,1)S(1)} fusion(f32[2,4,512]{2,1,0:T(4,128)S(1)} %fusion.1, f32[2,4,512]{2,1,0:T(4,128)S(1)} %get-tuple-element.8, f32[2,512,512,4]{2,1,3,0:T(8,128)} %get-tuple-element.9, pred[512,512]{0,1:T(8,128)(4,1)S(1)} %iota_compare_fusion, pred[2,4]{1,0:T(4,128)(4,1)S(1)} %eq.24, ...), kind=kOutput, calls=%fused_computation.23 | convolution fusion | flops 548405248 | bytes 10256392 | tf_op jit(solution)/shard_map/ekgtu,eukgd->etkgd/dot_general | solution.py:45
  318.0 1.3 copy.101
  (37 shorter events, 0.9 us)
Async XLA Ops:
  6.5 1.5 copy-start
  6.5 57.2 %all-gather.6.cloned.1.call-start = ((), (), s32[]{:S(2)}) async-start(), calls=%async_computation.5 | async-start | bytes 4456448 | tf_op jit(solution)/shard_map/all_gather | solution.py:94
  9.4 16.2 %copy-start.5 = (s32[32,16]{0,1:T(8,128)S(1)}, s32[32,16]{0,1:T(8,128)}, u32[]{:S(2)}) copy-start(s32[32,16]{0,1:T(8,128)} %param.16) | copy-start | bytes 6148
  12.2 32.8 %copy-start.3 = (bf16[1,1,512,1024]{3,2,1,0:T(8,128)(2,1)S(1)}, bf16[1,1,512,1024]{3,2,1,0:T(8,128)(2,1)}, u32[]{:S(2)}) copy-start(bf16[1,1,512,1024]{3,2,1,0:T(8,128)(2,1)} %param.14) | copy-start | bytes 3145732
  16.4 23.7 %all-to-all-start = ((bf16[16,2,4096]{2,1,0:T(2,128)(2,1)}), bf16[16,2,4096]{2,1,0:T(2,128)(2,1)S(1)}, u32[]{:S(2)}, u32[]{:S(2)}) async-start(bf16[16,2,4096]{2,1,0:T(2,128)(2,1)} %reshape.224), calls=%async_computation | async-start | bytes 524288 | tf_op jit(solution)/shard_map/all_to_all | solution.py:77
  41.5 17.7 %all-to-all-start.1 = ((bf16[16,32,256]{2,1,0:T(8,128)(2,1)}), bf16[16,32,256]{2,1,0:T(8,128)(2,1)S(1)}, u32[]{:S(2)}, u32[]{:S(2)}) async-start(bf16[16,32,256]{2,1,0:T(8,128)(2,1)} %copy.88), calls=%async_computation.1 | async-start | bytes 524288 | tf_op jit(solution)/shard_map/all_to_all | solution.py:83
  45.0 108.5 %reduce-scatter.2.cloned.1.call-start = ((), (), s32[]{:S(2)}) async-start(), calls=%async_computation.6 | async-start | bytes 10485760 | tf_op jit(solution)/shard_map/reduce_scatter | solution.py:97
  71.6 167.4 %all-gather.8.cloned.1.call-start = ((), (), s32[]{:S(2)}) async-start(), calls=%async_computation.7 | async-start | bytes 10485760 | tf_op jit(solution)/shard_map/all_gather | solution.py:100
  153.5 132.4 %all-gather.10.cloned.1.call-start = ((), (), s32[]{:S(2)}) async-start(), calls=%async_computation.8 | async-start | bytes 4456448 | tf_op jit(solution)/shard_map/all_gather | solution.py:114
  239.0 8.1 %copy-start.2 = (bf16[1,1,512,2048]{3,2,1,0:T(8,128)(2,1)S(1)}, bf16[1,1,512,2048]{3,2,1,0:T(8,128)(2,1)}, u32[]{:S(2)}) copy-start(bf16[1,1,512,2048]{3,2,1,0:T(8,128)(2,1)} %param.19) | copy-start | bytes 6291460
  245.1 1.9 copy-start.1
  247.1 6.1 %copy-start.6 = (bf16[1,2048]{1,0:T(2,128)(2,1)S(1)}, bf16[1,2048]{1,0:T(2,128)(2,1)}, u32[]{:S(2)}) copy-start(bf16[1,2048]{1,0:T(2,128)(2,1)} %param.20) | copy-start | bytes 12292
  248.3 9.2 %all-to-all-start.2 = ((f32[4,1,512]{2,1,0:T(1,128)}), f32[4,1,512]{2,1,0:T(1,128)S(1)}, u32[]{:S(2)}, u32[]{:S(2)}) async-start(f32[4,1,512]{2,1,0:T(1,128)} %broadcast_in_dim.86), calls=%async_computation.3 | async-start | bytes 16384 | tf_op jit(solution)/shard_map/all_to_all | solution.py:15
  291.8 5.2 %copy-start.4 = (bf16[512,2,4,128]{3,2,1,0:T(4,128)(2,1)S(1)}, bf16[512,2,4,128]{3,2,1,0:T(4,128)(2,1)}, u32[]{:S(2)}) copy-start(bf16[512,2,4,128]{3,2,1,0:T(4,128)(2,1)} %reshape.170) | copy-start | bytes 3145732
  292.9 18.7 %all-to-all-start.3 = ((bf16[4,512,256]{2,1,0:T(8,128)(2,1)}), bf16[4,512,256]{2,1,0:T(8,128)(2,1)S(1)}, u32[]{:S(2)}, u32[]{:S(2)}) async-start(bf16[4,512,256]{2,1,0:T(8,128)(2,1)} %bitcast.90), calls=%async_computation.4 | async-start | bytes 2097152 | tf_op jit(solution)/shard_map/all_to_all | solution.py:30
  297.0 6.8 %copy-start.7 = (s32[1,8]{1,0:T(1,128)S(1)}, s32[1,8]{1,0:T(1,128)}, u32[]{:S(2)}) copy-start(s32[1,8]{1,0:T(1,128)} %param.25) | copy-start | bytes 100
Sparse Core Ops, SparseCore 0:
  9.5 54.1 all-gather.5
  71.7 81.7 reduce-scatter.1
  155.3 83.6 all-gather.7
  240.7 45.2 all-gather.9
where the time goes:
time: 327 us; the launch traced here: 326 us
  waiting for transfers between devices  229 us (70%)
  matrix products  25.6 us (8%)
  starting transfers between devices  21.5 us (7%)
  local copies, waits for them, and re-layouts  19.2 us (6%)
  other arithmetic  16.9 us (5%)
  between operations  13.4 us (4%)
    all_gather x1, waiting for transfers between devices, per_device(): lax.all_gather(increment[None].astype(jnp.bfloat16), 'section', axis=0, t...  84.8 us
    reduce_scatter x1, waiting for transfers between devices, per_device(): lax.psum_scatter(partials.astype(jnp.bfloat16), 'tp', scatter_dimension=1...  81.9 us
    all_gather x1, waiting for transfers between devices, per_device(): lax.all_gather(value_weight[0], 'ex', axis=1, tiled=True)  28.4 us
    all_to_all x1, waiting for transfers between devices, per_device(): lax.all_to_all(corrupt, 'ex', split_axis=1, concat_axis=0, tiled=True)  14.4 us
    all_to_all x1, waiting for transfers between devices, per_device(): lax.all_to_all(patched, 'ex', split_axis=0, concat_axis=1, tiled=True)  12.3 us
    all_to_all x1, starting transfers between devices, per_device(): lax.all_to_all(corrupt, 'ex', split_axis=1, concat_axis=0, tiled=True)  9.15 us
    dot_general x1, matrix products, per_device(): jnp.dot(difference, lax.all_gather(weight_rows, 'ex', axis=1, tiled=True)...  7.78 us
  transfers between devices with their start and end apart: 8, of which 7 were waited for; matrix products, arithmetic and copies ran while one was open for 11% of the time, Pallas kernels for 0%

commit v1 on v0

v1 whole, which is shorter than its diff:
```python
import math

import jax
import jax.numpy as jnp
from jax import lax
from jax.sharding import PartitionSpec as P

D = 8192
HD = 128
GROUP = 4


def pick_columns(array, ids):
    parts = [lax.dynamic_slice_in_dim(array, ids[i] * HD, HD, 1) for i in range(ids.shape[0])]
    return jnp.concatenate(parts, axis=1)


def pick_rows(array, ids):
    parts = [lax.dynamic_slice_in_dim(array, ids[i] * HD, HD, 0) for i in range(ids.shape[0])]
    return jnp.concatenate(parts, axis=0)


def attend(queries, key_vectors, chosen):
    scores = jnp.einsum(
        "etkgd,eukd->ekgtu", queries, key_vectors, preferred_element_type=jnp.float32
    )
    scores = scores * (1.0 / math.sqrt(HD))
    places = jnp.arange(scores.shape[-1])
    causal = places[:, None] >= places[None, :]
    scores = jnp.where(causal, scores, -jnp.inf)
    maxima = jnp.max(scores, axis=-1, keepdims=True)
    exponent = jnp.exp(scores - maxima)
    weights = (exponent / jnp.sum(exponent, axis=-1, keepdims=True)).astype(jnp.bfloat16)
    return jnp.einsum("ekgtu,eukgd->etkgd", weights, chosen, preferred_element_type=jnp.float32)


def chunk_moves(sections, everyone, blocks):
    half = everyone // 2
    moves = []
    for r in range(sections):
        for j in range(everyone):
            for t in range(blocks):
                slot = blocks * r + t
                target_ex = 2 * (slot % half) + slot // half
                source = (r * everyone + j) * blocks + t
                target = ((j % sections) * everyone + target_ex) * blocks + j // sections
                moves.append((source, target))
    return moves


def over_chips(array, everyone):
    same_core = [list(range(c, everyone, 2)) for c in (0, 1)]
    same_chip = [[2 * i, 2 * i + 1] for i in range(everyone // 2)]
    one = lax.all_gather(array, "ex", axis_index_groups=same_core)
    return lax.all_gather(one, "ex", axis_index_groups=same_chip)


def per_device(
    clean_heads,
    corrupt_heads,
    donors,
    senders,
    out_weight,
    residual,
    norm_gain,
    value_weight,
    clean_values,
    queries,
    key_vectors,
    receivers,
):
    length = residual.shape[2]
    heads_here = clean_heads.shape[3] // HD
    sections = lax.axis_size("section")
    everyone = lax.axis_size("ex")
    blocks = lax.axis_size("tp")
    ids = senders[0] - lax.axis_index("tp") * heads_here
    corrupt = pick_columns(corrupt_heads[0, 0], ids)
    clean = pick_columns(clean_heads[0, 0], ids)
    rows = pick_rows(out_weight[0], ids)

    rows = lax.ppermute(rows, ("section", "ex", "tp"), chunk_moves(sections, everyone, blocks))
    weights = over_chips(rows, everyone).reshape(sections, blocks, *rows.shape)
    value_columns = over_chips(value_weight[0].T, everyone)
    value_columns = jnp.swapaxes(value_columns, 0, 1).reshape(-1, value_weight.shape[1])

    gathered = lax.all_to_all(corrupt[None], "ex", split_axis=1, concat_axis=0, tiled=True)
    onehot = (donors[:, :, None] == jnp.arange(everyone)[None, None, :]).astype(jnp.bfloat16)
    patched = jnp.einsum(
        "tef,ftc->etc", onehot, gathered, preferred_element_type=jnp.float32
    ).astype(jnp.bfloat16)
    returned = lax.all_to_all(patched, "ex", split_axis=0, concat_axis=1, tiled=True)[0]
    difference = (returned.astype(jnp.float32) - clean.astype(jnp.float32)).astype(jnp.bfloat16)

    differences = lax.all_gather(difference, ("section", "tp"))
    differences = differences.reshape(sections, blocks, *difference.shape)
    increments = jnp.einsum(
        "rtpk,rtkn->rpn", differences, weights, preferred_element_type=jnp.float32
    )
    running = [increments[0]]
    for r in range(1, sections):
        running.append(running[-1] + increments[r])
    carried = jnp.stack([c.astype(jnp.bfloat16) for c in running])
    carried = lax.all_to_all(carried, "section", 0, 0, tiled=True)
    width = carried.shape[-1]
    stream = residual[0, 0].reshape(length, sections, width).swapaxes(0, 1).astype(
        jnp.float32
    ) + carried.astype(jnp.float32)
    squares = jnp.sum(stream * stream, axis=(0, 2))
    gain = norm_gain[0].reshape(sections, 1, width).astype(jnp.float32)
    scaled = (stream * gain).astype(jnp.bfloat16)
    value_terms = jnp.einsum(
        "spc,nsc->pn",
        scaled,
        value_columns.reshape(-1, sections, width),
        preferred_element_type=jnp.float32,
    ).astype(jnp.bfloat16)
    per_block = value_terms.shape[1] // blocks
    pieces = jnp.moveaxis(value_terms.reshape(length, blocks, per_block), 1, 0)
    pieces = lax.all_to_all(pieces, "tp", 0, 0, tiled=True)
    squares = lax.all_to_all(
        jnp.broadcast_to(squares, (blocks, length)), "tp", 0, 0, tiled=True
    ).sum(axis=0)
    values = jnp.sum(pieces.astype(jnp.float32), axis=0)
    values = (values * lax.rsqrt(squares[:, None] / D + 1e-05)).astype(jnp.bfloat16)

    kv_here = values.shape[-1] // HD
    values = values.reshape(1, length, kv_here, 1, HD)
    clean_here = clean_values[0].reshape(1, length, kv_here, 1, HD)
    receive_flags = receivers[0].reshape(kv_here, GROUP)
    chosen = jnp.where((receive_flags == 1)[None, None, :, :, None], values, clean_here)
    attended = attend(
        queries[0].reshape(1, length, kv_here, GROUP, HD),
        key_vectors[0].reshape(1, length, kv_here, HD),
        chosen,
    )
    return attended.reshape(1, 1, length, -1).astype(jnp.bfloat16)


def solution(mesh):
    return jax.shard_map(
        per_device,
        mesh=mesh,
        in_specs=(
            P("section", "ex", None, "tp"),
            P("section", "ex", None, "tp"),
            P("ex", None),
            P("section", "tp"),
            P("section", "tp", "ex"),
            P("section", "ex", None, "tp"),
            P("section", "tp"),
            P("section", "tp", "ex"),
            P("section", "ex", None, "tp"),
            P("section", "ex", None, "tp"),
            P("section", "ex", None, "tp"),
            P("section", "tp"),
        ),
        out_specs=P("section", "ex", None, "tp"),
        check_vma=False,
    )
```

time: 327 us -> 303 us (0.927)
  waiting for transfers between devices: 229 us -> 181 us
  starting transfers between devices: 21.5 us -> 34.7 us
  local copies, waits for them, and re-layouts: 19.2 us -> 31.3 us
    reduce_scatter x1 -> x0, waiting for transfers between devices: 81.9 us -> none  [per_device(): lax.psum_scatter(partials.astype(jnp.bfloat16), 'tp', scatter_dimension=1...]
    all_gather x3 -> x5, waiting for transfers between devices: 117 us -> 132 us  [the longest x1 59.7 us: per_device(): differences = lax.all_gather(difference, ('section', 'tp'))]
    ppermute x0 -> x1, waiting for transfers between devices: none -> 13 us  [per_device(): lax.ppermute(rows, ('section', 'ex', 'tp'), chunk_moves(sections, everyon...]
    ppermute x0 -> x1, starting transfers between devices: none -> 9.66 us  [per_device(): lax.ppermute(rows, ('section', 'ex', 'tp'), chunk_moves(sections, everyon...]
    all_to_all x4 -> x5, waiting for transfers between devices: 29.4 us -> 34.9 us  [the longest x1 13.7 us: per_device(): lax.all_to_all(corrupt[None], 'ex', split_axis=1, concat_axis=0, tiled=True)]
    transpose x0 -> x1, local copies, waits for them, and re-layouts: none -> 4.72 us  [per_device(): jnp.swapaxes(value_columns, 0, 1).reshape(-1, value_weight.shape[1])]
    all_to_all x4 -> x5, starting transfers between devices: 21.4 us -> 24.9 us  [the longest x1 8.66 us: per_device(): lax.all_to_all(corrupt[None], 'ex', split_axis=1, concat_axis=0, tiled=True)]
    reduce_sum x4 -> x3, other arithmetic: 7.05 us -> 3.61 us  [the longest x1 3.44 us: per_device(): squares = jnp.sum(stream * stream, axis=(0, 2))]
  transfers between devices with their start and end apart: 8 -> 11, of which waited for: 7 -> 8; matrix products, arithmetic and copies ran while one was open for 11% -> 18% of each run, Pallas kernels for 0% -> 0%
where the time goes in v1:
time: 303 us; the launch traced here: 300 us
  waiting for transfers between devices  181 us (60%)
  starting transfers between devices  34.7 us (11%)
  local copies, waits for them, and re-layouts  31.3 us (10%)
  matrix products  23.3 us (8%)
  other arithmetic  14.9 us (5%)
  between operations  14.7 us (5%)
    all_gather x1, waiting for transfers between devices, per_device(): differences = lax.all_gather(difference, ('section', 'tp'))  59.7 us
    all_gather x2, waiting for transfers between devices, over_chips(): one = lax.all_gather(array, 'ex', axis_index_groups=same_core)  50.4 us
    all_gather x2, waiting for transfers between devices, over_chips(): return lax.all_gather(one, 'ex', axis_index_groups=same_chip)  22.1 us
    all_to_all x1, waiting for transfers between devices, per_device(): lax.all_to_all(corrupt[None], 'ex', split_axis=1, concat_axis=0, tiled=True)  13.7 us
    all_to_all x1, waiting for transfers between devices, per_device(): lax.all_to_all(patched, 'ex', split_axis=0, concat_axis=1, tiled=True)[0]  13 us
    ppermute x1, waiting for transfers between devices, per_device(): lax.ppermute(rows, ('section', 'ex', 'tp'), chunk_moves(sections, everyon...  13 us
    ppermute x1, starting transfers between devices, per_device(): lax.ppermute(rows, ('section', 'ex', 'tp'), chunk_moves(sections, everyon...  9.66 us
    all_to_all x1, starting transfers between devices, per_device(): lax.all_to_all(corrupt[None], 'ex', split_axis=1, concat_axis=0, tiled=True)  8.66 us
  transfers between devices with their start and end apart: 11, of which 8 were waited for; matrix products, arithmetic and copies ran while one was open for 18% of the time, Pallas kernels for 0%

profile of v1, /device:TPU:7, one launch (start us, length us, event | category | flops | bytes accessed | tf_op | source)
XLA Modules:
  0.0 299.8 jit_solution(7603864184552498135)
XLA Ops:
  6.5 0.7 broadcast_subtract_fusion
  7.2 0.6 fusion.29
  9.1 1.0 dynamic-slice_bitcast_fusion.1
  10.1 9.7 %collective-permute-start = (bf16[256,512]{1,0:T(8,128)(2,1)S(1)}, bf16[256,512]{1,0:T(8,128)(2,1)S(1)}, u32[]{:S(2)}, u32[]{:S(2)}) collective-permute-start(bf16[256,512]{1,0:T(8,128)(2,1)S(1)} %pad_maximum_fusion.1), channel_id=1, source_target_pairs={{0,0},{1,8},{2,16},{3,24},{4,64},{5,72},{6,80},{7,88},{8,128},{9,1... | collective-permute-start | bytes 786440 | tf_op jit(solution)/shard_map/ppermute | solution.py:82
  19.8 13.0 %collective-permute-done = bf16[256,512]{1,0:T(8,128)(2,1)S(1)} collective-permute-done((bf16[256,512]{1,0:T(8,128)(2,1)S(1)}, bf16[256,512]{1,0:T(8,128)(2,1)S(1)}, u32[]{:S(2)}, u32[]{:S(2)}) %collective-permute-start) | collective-permute-done | bytes 262176 | tf_op jit(solution)/shard_map/ppermute | solution.py:82
  32.8 0.7 copy-done.2
  33.6 0.7 all-gather.16.cloned.1.call-update
  34.3 46.5 %all-gather.12.cloned.1.call-done = bf16[2048,512]{1,0:T(8,128)(2,1)} async-done(((bf16[256,512]{1,0:T(8,128)(2,1)}), bf16[2048,512]{1,0:T(8,128)(2,1)}) %all-gather.12.cloned.1.call-update) | async-done | bytes 2097168 | tf_op jit(solution)/shard_map/all_gather | solution.py:54
  80.9 1.0 dynamic-slice_bitcast_fusion.5
  81.9 0.4 copy.169
  82.3 0.5 broadcast.62
  82.9 2.2 reduce.11
  85.1 0.8 reshape.210
  85.8 8.7 %all-to-all-start = ((bf16[16,2,4096]{2,1,0:T(2,128)(2,1)}), bf16[16,2,4096]{2,1,0:T(2,128)(2,1)S(1)}, u32[]{:S(2)}, u32[]{:S(2)}) async-start(bf16[16,2,4096]{2,1,0:T(2,128)(2,1)} %reshape.210), calls=%async_computation | async-start | bytes 524288 | tf_op jit(solution)/shard_map/all_to_all | solution.py:87
  94.6 13.7 %all-to-all-done = bf16[16,2,4096]{2,1,0:T(2,128)(2,1)S(1)} async-done(((bf16[16,2,4096]{2,1,0:T(2,128)(2,1)}), bf16[16,2,4096]{2,1,0:T(2,128)(2,1)S(1)}, u32[]{:S(2)}, u32[]{:S(2)}) %all-to-all-start) | async-done | bytes 262176 | tf_op jit(solution)/shard_map/all_to_all | solution.py:87
  108.3 0.3 reshape.211
  108.6 0.3 fusion.13
  108.9 0.8 copy.128
  109.7 3.4 %all-to-all-start.1 = ((bf16[16,32,256]{2,1,0:T(8,128)(2,1)}), bf16[16,32,256]{2,1,0:T(8,128)(2,1)S(1)}, u32[]{:S(2)}, u32[]{:S(2)}) async-start(bf16[16,32,256]{2,1,0:T(8,128)(2,1)} %copy.128), calls=%async_computation.1 | async-start | bytes 524288 | tf_op jit(solution)/shard_map/all_to_all | solution.py:92
  113.2 1.0 dynamic-slice_bitcast_fusion.3
  114.2 13.0 %all-to-all-done.1 = bf16[16,32,256]{2,1,0:T(8,128)(2,1)S(1)} async-done(((bf16[16,32,256]{2,1,0:T(8,128)(2,1)}), bf16[16,32,256]{2,1,0:T(8,128)(2,1)S(1)}, u32[]{:S(2)}, u32[]{:S(2)}) %all-to-all-start.1) | async-done | bytes 262176 | tf_op jit(solution)/shard_map/all_to_all | solution.py:92
  127.2 0.8 fusion.19
  128.0 3.8 %all-gather.16.cloned.1.call-done = bf16[512,2048]{1,0:T(8,128)(2,1)} async-done(((bf16[64,2048]{1,0:T(8,128)(2,1)}), bf16[512,2048]{1,0:T(8,128)(2,1)}) %all-gather.16.cloned.1.call-update) | async-done | bytes 2097168 | tf_op jit(solution)/shard_map/all_gather | solution.py:54
  131.9 22.1 %all-gather.14.cloned.1.call-done = bf16[16,256,512]{2,1,0:T(8,128)(2,1)} async-done(((bf16[8,256,512]{2,1,0:T(8,128)(2,1)}), bf16[16,256,512]{2,1,0:T(8,128)(2,1)}) %all-gather.14.cloned.1.call-update) | async-done | bytes 4194320 | tf_op jit(solution)/shard_map/all_gather | solution.py:55
  154.0 59.7 %all-gather.10.cloned.1.call-done = bf16[16,512,256]{2,1,0:T(8,128)(2,1)} async-done(((bf16[1,512,256]{2,1,0:T(8,128)(2,1)}), bf16[16,512,256]{2,1,0:T(8,128)(2,1)}) %all-gather.10.cloned.1.call-update) | async-done | bytes 4194320 | tf_op jit(solution)/shard_map/all_gather | solution.py:95
  213.7 5.8 %convolution_bitcast_fusion = f32[4,512,512]{2,1,0:T(8,128)S(1)} fusion(bf16[4,4,512,256]{3,2,1,0:T(8,128)(2,1)} %bitcast.111, bf16[4,4,256,512]{3,2,1,0:T(8,128)(2,1)} %bitcast.110), kind=kOutput, calls=%fused_computation.13 | convolution fusion | flops 2147483648 | bytes 12582912 | tf_op jit(solution)/shard_map/rtpk,rtkn->rpn/dot_general | solution.py:97
  219.6 0.6 fusion.28
  220.1 1.6 pad_maximum_fusion
  221.7 4.7 %all-to-all-start.2 = ((bf16[4,512,512]{2,1,0:T(8,128)(2,1)}), bf16[4,512,512]{2,1,0:T(8,128)(2,1)}, u32[]{:S(2)}, u32[]{:S(2)}) async-start(bf16[4,512,512]{2,1,0:T(8,128)(2,1)} %pad_maximum_fusion), calls=%async_computation.2 | async-start | bytes 4194304 | tf_op jit(solution)/shard_map/all_to_all | solution.py:104
  226.4 3.0 %copy.123 = bf16[1,1,512,2048]{2,3,1,0:T(8,128)(2,1)S(1)} copy(bf16[1,1,512,2048]{3,2,1,0:T(8,128)(2,1)} %param.17) | data formatting | bytes 4194304 | tf_op args[5]
  229.5 2.9 copy.124
  232.5 0.8 reshape.183
  233.3 1.1 copy.145
  234.6 4.8 %fusion.1 = (f32[2,4,512]{2,1,0:T(4,128)S(1)}, f32[2,512,512,4]{2,1,3,0:T(8,128)}) fusion(pred[512,512]{0,1:T(8,128)(4,1)S(1)} %iota_compare_fusion, bf16[512,2,4,128]{3,2,1,0:T(4,128)(2,1)S(1)} %reshape.183, bf16[512,2,128,1]{2,1,0,3:T(2,128)(2,1)S(1)} %bitcast.109), kind=kOutput, calls=%fused_computation.4 | convolution fusion | flops 543158272 | bytes 9977856 | tf_op jit(solution)/shard_map/etkgd,eukd->ekgtu/dot_general | solution.py:24
  239.4 4.7 %copy.129 = bf16[8,2,64,2048]{3,2,1,0:T(8,128)(2,1)} copy(bf16[8,2,64,2048]{3,2,0,1:T(8,128)(2,1)} %bitcast.97) | data formatting | bytes 8388608 | tf_op jit(solution)/shard_map/transpose | solution.py:85
  244.2 7.8 %reshape_reshape.3 = bf16[1024,4,512]{2,1,0:T(4,128)(2,1)} reshape(bf16[8,2,64,2048]{3,2,1,0:T(8,128)(2,1)} %copy.129) | data formatting | bytes 8388608 | tf_op jit(solution)/shard_map/reshape;reshape | solution.py:115
  252.0 3.4 %multiply_reduce_fusion = f32[512]{0:T(512)S(1)} fusion(bf16[4,512,512]{2,1,0:T(8,128)(2,1)} %all-to-all-done.2, f32[512,4,512]{2,0,1:T(8,128)} %copy.124), kind=kLoop, calls=%fused_computation.10 | loop fusion | flops 4193792 | bytes 6293504 | tf_op jit(solution)/shard_map/reduce_sum | solution.py:109
  255.5 0.6 broadcast_in_dim.50
  256.1 3.9 %all-to-all-start.4 = ((f32[4,1,512]{2,1,0:T(1,128)}), f32[4,1,512]{2,1,0:T(1,128)S(1)}, u32[]{:S(2)}, u32[]{:S(2)}) async-start(f32[4,1,512]{2,1,0:T(1,128)} %broadcast_in_dim.50), calls=%async_computation.4 | async-start | bytes 16384 | tf_op jit(solution)/shard_map/all_to_all | solution.py:121
  260.0 6.6 %bitcast_convert_fusion = bf16[512,1024]{1,0:T(8,128)(2,1)S(1)} fusion(bf16[1024,4,512]{2,1,0:T(4,128)(2,1)} %reshape_reshape.3, bf16[4,512,512]{2,1,0:T(8,128)(2,1)} %all-to-all-done.2, f32[512,4,512]{2,0,1:T(8,128)} %copy.124, f32[4,512]{1,0:T(4,128)S(1)} %reshape.186), kind=kOutput, calls=%fused_computation.15 | convolution fusion | flops 2152202240 | bytes 11542528 | tf_op jit(solution)/shard_map/spc,nsc->pn/dot_general | solution.py:112
  266.5 1.0 copy.168
  267.6 4.2 %all-to-all-start.3 = ((bf16[4,512,256]{2,1,0:T(8,128)(2,1)}), bf16[4,512,256]{2,1,0:T(8,128)(2,1)S(1)}, u32[]{:S(2)}, u32[]{:S(2)}) async-start(bf16[4,512,256]{2,1,0:T(8,128)(2,1)} %bitcast.93), calls=%async_computation.3 | async-start | bytes 2097152 | tf_op jit(solution)/shard_map/all_to_all | solution.py:120
  271.8 5.1 %fusion = f32[2,4,512]{2,1,0:T(4,128)S(1)} fusion(f32[2,512,512,4]{2,1,3,0:T(8,128)} %get-tuple-element.17, f32[2,4,512]{2,1,0:T(4,128)S(1)} %get-tuple-element.16, pred[512,512]{0,1:T(8,128)(4,1)S(1)} %iota_compare_fusion), kind=kLoop, calls=%fused_computation.3 | loop fusion | flops 8384512 | bytes 8683520 | tf_op jit(solution)/shard_map/reduce_sum | solution.py:33
  277.0 8.2 %all-to-all-done.3 = bf16[4,512,256]{2,1,0:T(8,128)(2,1)S(1)} async-done(((bf16[4,512,256]{2,1,0:T(8,128)(2,1)}), bf16[4,512,256]{2,1,0:T(8,128)(2,1)S(1)}, u32[]{:S(2)}, u32[]{:S(2)}) %all-to-all-start.3) | async-done | bytes 1048608 | tf_op jit(solution)/shard_map/all_to_all | solution.py:120
  285.3 0.2 copy.133
  285.5 0.2 copy.135
  286.0 5.9 %fusion.10 = bf16[2,4,128,512]{3,2,1,0:T(8,128)(2,1)S(1)} fusion(f32[2,4,512]{2,1,0:T(4,128)S(1)} %fusion, f32[2,4,512]{2,1,0:T(4,128)S(1)} %get-tuple-element.16, f32[2,512,512,4]{2,1,3,0:T(8,128)} %get-tuple-element.17, pred[512,512]{0,1:T(8,128)(4,1)S(1)} %iota_compare_fusion, pred[2,4]{1,0:T(4,128)(4,1)S(1)} %eq.24, ...), kind=kOutput, calls=%fused_computation.18 | convolution fusion | flops 548405248 | bytes 10256392 | tf_op jit(solution)/shard_map/ekgtu,eukgd->etkgd/dot_general | solution.py:34
  291.9 1.3 copy.141
  (39 shorter events, 1.3 us)
Async XLA Ops:
  6.5 88.0 %copy-start.3 = (s32[32,16]{0,1:T(8,128)S(1)}, s32[32,16]{0,1:T(8,128)}, u32[]{:S(2)}) copy-start(s32[32,16]{0,1:T(8,128)} %param.14) | copy-start | bytes 6148
  6.5 74.3 %all-gather.12.cloned.1.call-start = ((), (), s32[]{:S(2)}) async-start(), calls=%async_computation.6 | async-start | bytes 2359296 | tf_op jit(solution)/shard_map/all_gather | solution.py:54
  10.1 22.7 %collective-permute-start = (bf16[256,512]{1,0:T(8,128)(2,1)S(1)}, bf16[256,512]{1,0:T(8,128)(2,1)S(1)}, u32[]{:S(2)}, u32[]{:S(2)}) collective-permute-start(bf16[256,512]{1,0:T(8,128)(2,1)S(1)} %pad_maximum_fusion.1), channel_id=1, source_target_pairs={{0,0},{1,8},{2,16},{3,24},{4,64},{5,72},{6,80},{7,88},{8,128},{9,1... | collective-permute-start | bytes 786440 | tf_op jit(solution)/shard_map/ppermute | solution.py:82
  32.8 0.7 copy-start.2
  33.5 98.3 %all-gather.16.cloned.1.call-start = ((), (), s32[]{:S(2)}) async-start(), calls=%async_computation.8 | async-start | bytes 2359296 | tf_op jit(solution)/shard_map/all_gather | solution.py:54
  34.3 119.7 %all-gather.14.cloned.1.call-start = ((), (), s32[]{:S(2)}) async-start(), calls=%async_computation.7 | async-start | bytes 6291456 | tf_op jit(solution)/shard_map/all_gather | solution.py:55
  85.8 22.4 %all-to-all-start = ((bf16[16,2,4096]{2,1,0:T(2,128)(2,1)}), bf16[16,2,4096]{2,1,0:T(2,128)(2,1)S(1)}, u32[]{:S(2)}, u32[]{:S(2)}) async-start(bf16[16,2,4096]{2,1,0:T(2,128)(2,1)} %reshape.210), calls=%async_computation | async-start | bytes 524288 | tf_op jit(solution)/shard_map/all_to_all | solution.py:87
  109.7 17.5 %all-to-all-start.1 = ((bf16[16,32,256]{2,1,0:T(8,128)(2,1)}), bf16[16,32,256]{2,1,0:T(8,128)(2,1)S(1)}, u32[]{:S(2)}, u32[]{:S(2)}) async-start(bf16[16,32,256]{2,1,0:T(8,128)(2,1)} %copy.128), calls=%async_computation.1 | async-start | bytes 524288 | tf_op jit(solution)/shard_map/all_to_all | solution.py:92
  113.1 100.6 %all-gather.10.cloned.1.call-start = ((), (), s32[]{:S(2)}) async-start(), calls=%async_computation.5 | async-start | bytes 4456448 | tf_op jit(solution)/shard_map/all_gather | solution.py:95
  128.0 111.4 %all-gather.18.cloned.1.call-start = ((), (), s32[]{:S(2)}) async-start(), calls=%async_computation.9 | async-start | bytes 6291456 | tf_op jit(solution)/shard_map/all_gather | solution.py:55
  221.7 30.3 %all-to-all-start.2 = ((bf16[4,512,512]{2,1,0:T(8,128)(2,1)}), bf16[4,512,512]{2,1,0:T(8,128)(2,1)}, u32[]{:S(2)}, u32[]{:S(2)}) async-start(bf16[4,512,512]{2,1,0:T(8,128)(2,1)} %pad_maximum_fusion), calls=%async_computation.2 | async-start | bytes 4194304 | tf_op jit(solution)/shard_map/all_to_all | solution.py:104
  229.5 3.0 copy-start.4
  229.5 3.0 %copy-start = (bf16[1,1,512,1024]{3,2,1,0:T(8,128)(2,1)S(1)}, bf16[1,1,512,1024]{3,2,1,0:T(8,128)(2,1)}, u32[]{:S(2)}) copy-start(bf16[1,1,512,1024]{3,2,1,0:T(8,128)(2,1)} %param.21) | copy-start | bytes 3145732
  229.5 3.8 %copy-start.1 = (bf16[1,1,512,256]{3,2,1,0:T(8,128)(2,1)S(1)}, bf16[1,1,512,256]{3,2,1,0:T(8,128)(2,1)}, u32[]{:S(2)}) copy-start(bf16[1,1,512,256]{3,2,1,0:T(8,128)(2,1)} %param.22) | copy-start | bytes 786436
  229.5 4.9 %copy-start.5 = (s32[1,8]{1,0:T(1,128)S(1)}, s32[1,8]{1,0:T(1,128)}, u32[]{:S(2)}) copy-start(s32[1,8]{1,0:T(1,128)} %param.23) | copy-start | bytes 100
  256.1 11.5 %all-to-all-start.4 = ((f32[4,1,512]{2,1,0:T(1,128)}), f32[4,1,512]{2,1,0:T(1,128)S(1)}, u32[]{:S(2)}, u32[]{:S(2)}) async-start(f32[4,1,512]{2,1,0:T(1,128)} %broadcast_in_dim.50), calls=%async_computation.4 | async-start | bytes 16384 | tf_op jit(solution)/shard_map/all_to_all | solution.py:121
  267.6 17.6 %all-to-all-start.3 = ((bf16[4,512,256]{2,1,0:T(8,128)(2,1)}), bf16[4,512,256]{2,1,0:T(8,128)(2,1)S(1)}, u32[]{:S(2)}, u32[]{:S(2)}) async-start(bf16[4,512,256]{2,1,0:T(8,128)(2,1)} %bitcast.93), calls=%async_computation.3 | async-start | bytes 2097152 | tf_op jit(solution)/shard_map/all_to_all | solution.py:120
Sparse Core Ops, SparseCore 0:
  33.7 47.1 all-gather.11
  82.7 49.1 all-gather.15
  133.7 20.2 all-gather.13
  156.3 57.3 all-gather.9
  215.3 19.1 all-gather.17

commit v2 on v1

v2 whole, which is shorter than its diff:
```python
import math

import jax
import jax.numpy as jnp
from jax import lax
from jax.experimental import pallas as pl
from jax.experimental.pallas import tpu as pltpu
from jax.sharding import PartitionSpec as P

D = 8192
HD = 128
GROUP = 4
SEC = 4
EX = 16
TP = 4
ROWS = 512
HALF = 256
BF = jnp.bfloat16
F32 = jnp.float32
MESH = pl.DeviceIdType.MESH
CHIPS = EX // 2


def dot_nt(a, b):
    return lax.dot_general(a, b, (((1,), (1,)), ((), ())), preferred_element_type=F32)


def remote(src, dst, send, recv, device):
    return pltpu.make_async_remote_copy(
        src_ref=src,
        dst_ref=dst,
        send_sem=send,
        recv_sem=recv,
        device_id=device,
        device_id_type=MESH,
    )


def kernel(
    corrupt,
    clean,
    target,
    weight,
    value_weight,
    flags,
    gain,
    residual_hbm,
    clean_values_hbm,
    queries_hbm,
    keys_hbm,
    out,
    arrived,
    patched,
    returned,
    weights,
    value_weights,
    differences,
    total,
    carried_out,
    carried_in,
    scaled,
    values_out,
    values_in,
    squares_out,
    squares_in,
    values,
    probabilities,
    residual,
    clean_values,
    queries,
    keys,
    local_sem,
    patch_send,
    patch_recv,
    back_send,
    back_recv,
    piece_send,
    piece_recv,
    up_send,
    up_recv,
    down_send,
    down_recv,
    side_send,
    side_recv,
    diff_send,
    diff_recv,
    carry_send,
    carry_recv,
    value_send,
    value_recv,
    square_send,
    square_recv,
):
    sec = lax.axis_index("section")
    ex = lax.axis_index("ex")
    tp = lax.axis_index("tp")
    chip = ex // 2
    core = lax.rem(ex, 2)
    mine = TP * sec + tp
    group = SEC * tp + sec

    loads = [
        pltpu.make_async_copy(queries_hbm, queries, local_sem.at[0]),
        pltpu.make_async_copy(keys_hbm, keys, local_sem.at[1]),
        pltpu.make_async_copy(residual_hbm, residual, local_sem.at[2]),
        pltpu.make_async_copy(clean_values_hbm, clean_values, local_sem.at[3]),
    ]
    for load in loads:
        load.start()

    barrier = pltpu.get_barrier_semaphore()

    @pl.loop(1, EX)
    def _(i):
        pl.semaphore_signal(
            barrier, inc=1, device_id={"ex": lax.rem(ex + i, EX)}, device_id_type=MESH
        )

    def plane_peer(i):
        other = lax.rem(mine + i, EX)
        return other // TP, lax.rem(other, TP)

    @pl.loop(1, EX)
    def _(i):
        s, t = plane_peer(i)
        pl.semaphore_signal(
            barrier, inc=1, device_id={"section": s, "tp": t}, device_id_type=MESH
        )

    pl.semaphore_wait(barrier, 2 * (EX - 1))

    @pl.loop(1, EX)
    def _(i):
        other = lax.rem(ex + i, EX)
        remote(
            corrupt.at[other], arrived.at[ex], patch_send.at[i], patch_recv.at[ex], {"ex": other}
        ).start()

    @pl.loop(1, EX)
    def _(i):
        s, t = plane_peer(i)
        remote(
            weight.at[SEC * t + s],
            weights.at[ex, mine],
            piece_send.at[i],
            piece_recv.at[mine],
            {"section": s, "tp": t},
        ).start()

    arrived[ex] = corrupt[ex]
    weights[ex, mine] = weight[group]
    value_weights[ex] = value_weight[...]

    def ring_start(which, buffer):
        block = buffer.at[ex]
        up = 2 * lax.rem(chip + 1, CHIPS) + core
        down = 2 * lax.rem(chip + CHIPS - 1, CHIPS) + core
        remote(block, block, up_send.at[which, 0], up_recv.at[which, 0], {"ex": up}).start()
        remote(block, block, down_send.at[which, 0], down_recv.at[which, 0], {"ex": down}).start()
        remote(
            block, block, side_send.at[which, 0], side_recv.at[which, 0], {"ex": 2 * chip + 1 - core}
        ).start()

    def ring_relay(which, buffer, step):
        up = 2 * lax.rem(chip + 1, CHIPS) + core
        down = 2 * lax.rem(chip + CHIPS - 1, CHIPS) + core
        side = 2 * chip + 1 - core
        block = buffer.at[2 * lax.rem(chip + CHIPS - step, CHIPS) + core]
        remote(
            block, block, up_send.at[which, step - 1], up_recv.at[which, step - 1], {"ex": up}
        ).wait_recv()
        if step < 4:
            remote(
                block, block, up_send.at[which, step], up_recv.at[which, step], {"ex": up}
            ).start()
        remote(
            block, block, side_send.at[which, step], side_recv.at[which, step], {"ex": side}
        ).start()
        if step < 4:
            block = buffer.at[2 * lax.rem(chip + step, CHIPS) + core]
            remote(
                block,
                block,
                down_send.at[which, step - 1],
                down_recv.at[which, step - 1],
                {"ex": down},
            ).wait_recv()
            if step < 3:
                remote(
                    block, block, down_send.at[which, step], down_recv.at[which, step], {"ex": down}
                ).start()
            remote(
                block,
                block,
                side_send.at[which, 4 + step],
                side_recv.at[which, 4 + step],
                {"ex": side},
            ).start()

    def ring_finish(which, buffer):
        side = 2 * chip + 1 - core
        for step in range(8):
            shift = CHIPS - step if step < 5 else step - 4
            block = buffer.at[2 * lax.rem(chip + shift, CHIPS) + 1 - core]
            remote(
                block, block, side_send.at[which, step], side_recv.at[which, step], {"ex": side}
            ).wait_recv()

    def ring_drain(which, buffer):
        block = buffer.at[ex]
        for step in range(4):
            remote(
                block, block, up_send.at[which, step], up_recv.at[which, step], {"ex": 0}
            ).wait_send()
        for step in range(3):
            remote(
                block, block, down_send.at[which, step], down_recv.at[which, step], {"ex": 0}
            ).wait_send()
        for step in range(8):
            remote(
                block, block, side_send.at[which, step], side_recv.at[which, step], {"ex": 0}
            ).wait_send()

    def softmax(scores):
        exponent = jnp.exp(scores - jnp.max(scores, axis=-1, keepdims=True))
        return (exponent / jnp.sum(exponent, axis=-1, keepdims=True)).astype(BF)

    def weigh_heads(low, high):
        @pl.loop(low, high)
        def _(h):
            lanes = pl.ds(pl.multiple_of(h * HD, HD), HD)
            shared = pl.ds(pl.multiple_of(h // GROUP * HD, HD), HD)
            for half in (0, 1):
                length = HALF * (half + 1)
                scores = dot_nt(
                    queries[half * HALF : (half + 1) * HALF, lanes], keys[:length, shared]
                ) * (1.0 / math.sqrt(HD))
                row = lax.broadcasted_iota(jnp.int32, scores.shape, 0) + half * HALF
                column = lax.broadcasted_iota(jnp.int32, scores.shape, 1)
                scores = jnp.where(row >= column, scores, -jnp.inf)
                probabilities[h, half * HALF : (half + 1) * HALF, :length] = softmax(scores)

    loads[0].wait()
    loads[1].wait()
    weigh_heads(0, 1)

    @pl.loop(1, EX)
    def _(i):
        other = lax.rem(mine + i, EX)
        remote(
            weights.at[ex, other],
            weights.at[ex, other],
            piece_send.at[i],
            piece_recv.at[other],
            {"ex": ex},
        ).wait_recv()

    ring_start(0, weights)

    @pl.loop(1, EX)
    def _(i):
        other = lax.rem(ex + i, EX)
        remote(
            arrived.at[other], arrived.at[other], patch_send.at[i], patch_recv.at[other], {"ex": other}
        ).wait_recv()

    column = lax.broadcasted_iota(jnp.int32, (ROWS, ROWS), 1)
    onehot = (column == target[...]).astype(F32).astype(BF)
    moved = jnp.dot(
        onehot, arrived[...].reshape(ROWS, 2 * HD), preferred_element_type=F32
    ).astype(BF)
    patched[...] = moved.reshape(EX, ROWS // EX, 2 * HD)

    @pl.loop(1, EX)
    def _(i):
        other = lax.rem(ex + i, EX)
        remote(
            patched.at[other], returned.at[ex], back_send.at[i], back_recv.at[ex], {"ex": other}
        ).start()

    returned[ex] = patched[ex]
    weigh_heads(1, 3)

    @pl.loop(1, EX)
    def _(i):
        other = lax.rem(ex + i, EX)
        remote(
            returned.at[other],
            returned.at[other],
            back_send.at[i],
            back_recv.at[other],
            {"ex": other},
        ).wait_recv()

    change = returned[...].reshape(ROWS, 2 * HD).astype(F32) - clean[...].astype(F32)
    differences[0, mine] = change[:HALF].astype(BF)
    differences[1, mine] = change[HALF:].astype(BF)

    def along(axis, half, block, slot):
        here = sec if axis == "section" else tp
        for i in range(1, 4):
            ref = differences.at[half, block]
            remote(
                ref,
                ref,
                diff_send.at[half, slot + i - 1],
                diff_recv.at[half, block],
                {axis: lax.rem(here + i, 4)},
            ).start()

    def difference_wait(half, block):
        ref = differences.at[half, block]
        remote(ref, ref, diff_send.at[half, 0], diff_recv.at[half, block], {"ex": ex}).wait_recv()

    along("tp", 0, mine, 0)
    along("section", 1, mine, 0)
    along("section", 0, mine, 3)
    along("tp", 1, mine, 3)
    ring_relay(0, weights, 1)
    for i in range(1, 4):
        block = TP * sec + lax.rem(tp + i, TP)
        difference_wait(0, block)
        along("section", 0, block, 3 + 3 * i)
        block = TP * lax.rem(sec + i, SEC) + tp
        difference_wait(1, block)
        along("tp", 1, block, 3 + 3 * i)
    ring_relay(0, weights, 2)
    weigh_heads(3, 5)
    ring_relay(0, weights, 3)
    ring_start(1, value_weights)
    weigh_heads(5, 7)
    ring_relay(0, weights, 4)
    ring_finish(0, weights)

    def carry(half):
        @pl.loop(0, SEC)
        def _(r):
            for t in range(TP):
                block = TP * r + t
                first = (block // TP == sec) if half == 0 else (t == tp)
                @pl.when(jnp.logical_not(first))
                def _():
                    difference_wait(half, block)

            term = dot_nt(differences[half, TP * r], weights[:, TP * r].reshape(ROWS, 2 * HD))
            for t in range(1, TP):
                term += dot_nt(
                    differences[half, TP * r + t], weights[:, TP * r + t].reshape(ROWS, 2 * HD)
                )

            @pl.when(r == 0)
            def _():
                total[...] = term

            @pl.when(r > 0)
            def _():
                total[...] += term

            rounded = total[...].astype(BF)
            for t in range(TP):
                carried_out[half, r, t] = rounded[:, t * HD : (t + 1) * HD]
                here = jnp.logical_and(r == sec, t == tp)

                @pl.when(here)
                def _():
                    carried_in[half, group] = carried_out[half, r, t]

                @pl.when(jnp.logical_not(here))
                def _():
                    remote(
                        carried_out.at[half, r, t],
                        carried_in.at[half, group],
                        carry_send.at[half, TP * r + t],
                        carry_recv.at[half, group],
                        {"section": r, "tp": t},
                    ).start()

    carry(0)
    ring_relay(1, value_weights, 1)
    carry(1)
    ring_relay(1, value_weights, 2)
    weigh_heads(7, 8)
    ring_relay(1, value_weights, 3)
    ring_relay(1, value_weights, 4)
    ring_finish(1, value_weights)
    loads[2].wait()
    loads[3].wait()

    source = lax.broadcasted_iota(jnp.int32, (ROWS, ROWS), 0)
    column = lax.broadcasted_iota(jnp.int32, (ROWS, ROWS), 1)
    place = source // 32 % 4 * 128 + source // 128 * 32 + source % 32
    order = (place == column).astype(F32).astype(BF)

    def finish_stream(half):
        rows = slice(half * HALF, (half + 1) * HALF)

        @pl.loop(1, EX)
        def _(i):
            other = lax.rem(group + i, EX)
            remote(
                carried_in.at[half, other],
                carried_in.at[half, other],
                carry_send.at[half, 0],
                carry_recv.at[half, other],
                {"ex": ex},
            ).wait_recv()

        square = jnp.zeros((HALF, HD), F32)
        for g in range(4):
            pieces = jnp.concatenate([carried_in[half, 4 * g + q] for q in range(4)], axis=1)
            ordered = jnp.dot(pieces, order, preferred_element_type=F32)
            for j in range(4):
                lanes = slice(j * ROWS + g * HD, j * ROWS + (g + 1) * HD)
                stream = residual[rows, lanes].astype(F32) + ordered[:, j * HD : (j + 1) * HD]
                square += stream * stream
                scaled[rows, lanes] = (stream * gain[:, lanes].astype(F32)).astype(BF)
        sums = jnp.broadcast_to(jnp.sum(square, axis=1, keepdims=True), (HALF, HD))
        squares_out[half] = jnp.transpose(sums)[:8]
        squares_in[half, tp] = squares_out[half]
        for i in range(1, TP):
            other = lax.rem(tp + i, TP)
            remote(
                squares_out.at[half],
                squares_in.at[half, tp],
                square_send.at[half, i],
                square_recv.at[half, tp],
                {"tp": other},
            ).start()

        @pl.loop(1, TP + 1)
        def _(i):
            other = lax.rem(tp + i, TP)
            columns = value_weights[pl.ds(4 * other, 4)].reshape(2 * HD, SEC * ROWS)
            values_out[half, other] = dot_nt(scaled[rows, :], columns).astype(BF)

            @pl.when(i < TP)
            def _():
                remote(
                    values_out.at[half, other],
                    values_in.at[half, tp],
                    value_send.at[half, other],
                    value_recv.at[half, tp],
                    {"tp": other},
                ).start()

        values_in[half, tp] = values_out[half, tp]

    def attend(half):
        rows = slice(half * HALF, (half + 1) * HALF)
        for i in range(1, TP):
            other = lax.rem(tp + i, TP)
            remote(
                values_in.at[half, other],
                values_in.at[half, other],
                value_send.at[half, 0],
                value_recv.at[half, other],
                {"ex": ex},
            ).wait_recv()
            remote(
                squares_in.at[half, other],
                squares_in.at[half, other],
                square_send.at[half, 0],
                square_recv.at[half, other],
                {"ex": ex},
            ).wait_recv()
        squares = (squares_in[half, 0] + squares_in[half, 1]) + (
            squares_in[half, 2] + squares_in[half, 3]
        )
        scale = lax.rsqrt(squares / D + 1e-05)
        scale = jnp.transpose(jnp.concatenate([scale] * 16, axis=0))
        for g in (0, 1):
            lanes = slice(g * HD, (g + 1) * HD)
            summed = values_in[half, 0, :, lanes].astype(F32)
            for t in range(1, TP):
                summed += values_in[half, t, :, lanes].astype(F32)
            values[rows, lanes] = (summed * scale).astype(BF)
        length = HALF * (half + 1)

        @pl.loop(0, 2 * GROUP)
        def _(h):
            shared = pl.ds(pl.multiple_of(h // GROUP * HD, HD), HD)
            flag = jnp.broadcast_to(flags[pl.ds(h, 1), :], (length, HD)) == 1
            chosen = jnp.where(
                flag,
                values[:length, shared].astype(F32),
                clean_values[:length, shared].astype(F32),
            ).astype(BF)
            out[rows, pl.ds(pl.multiple_of(h * HD, HD), HD)] = jnp.dot(
                probabilities[h, rows, :length], chosen, preferred_element_type=F32
            ).astype(BF)

    finish_stream(0)
    finish_stream(1)
    attend(0)
    attend(1)

    @pl.loop(1, EX)
    def _(i):
        remote(corrupt.at[0], arrived.at[0], patch_send.at[i], patch_recv.at[0], {"ex": 0}).wait_send()
        remote(patched.at[0], returned.at[0], back_send.at[i], back_recv.at[0], {"ex": 0}).wait_send()
        remote(
            weight.at[0], weights.at[0, 0], piece_send.at[i], piece_recv.at[0], {"ex": 0}
        ).wait_send()

    ring_drain(0, weights)
    ring_drain(1, value_weights)
    for half in (0, 1):

        @pl.loop(0, EX - 1)
        def _(i):
            ref = differences.at[half, 0]
            remote(ref, ref, diff_send.at[half, i], diff_recv.at[half, 0], {"ex": 0}).wait_send()

        @pl.loop(1, EX)
        def _(i):
            other = lax.rem(mine + i, EX)
            remote(
                carried_out.at[half, 0, 0],
                carried_in.at[half, 0],
                carry_send.at[half, other],
                carry_recv.at[half, 0],
                {"ex": 0},
            ).wait_send()

        for i in range(1, TP):
            other = lax.rem(tp + i, TP)
            remote(
                values_out.at[half, 0],
                values_in.at[half, 0],
                value_send.at[half, other],
                value_recv.at[half, 0],
                {"ex": 0},
            ).wait_send()
            remote(
                squares_out.at[half],
                squares_in.at[half, 0],
                square_send.at[half, i],
                square_recv.at[half, 0],
                {"ex": 0},
            ).wait_send()


def pick_columns(array, ids):
    parts = [lax.dynamic_slice_in_dim(array, ids[i] * HD, HD, 1) for i in range(ids.shape[0])]
    return jnp.concatenate(parts, axis=1)


def pick_rows(array, ids):
    parts = [lax.dynamic_slice_in_dim(array, ids[i] * HD, HD, 0) for i in range(ids.shape[0])]
    return jnp.concatenate(parts, axis=0)


def per_device(
    clean_heads,
    corrupt_heads,
    donors,
    senders,
    out_weight,
    residual,
    norm_gain,
    value_weight,
    clean_values,
    queries,
    key_vectors,
    receivers,
):
    heads_here = clean_heads.shape[3] // HD
    ids = senders[0] - lax.axis_index("tp") * heads_here
    corrupt = pick_columns(corrupt_heads[0, 0], ids).reshape(EX, ROWS // EX, 2 * HD)
    clean = pick_columns(clean_heads[0, 0], ids)
    weight = pick_rows(out_weight[0], ids).T.reshape(EX, ROWS // EX, 2 * HD)
    block = ROWS // EX
    target = (donors.T * block + jnp.arange(block, dtype=jnp.int32)[None, :]).reshape(ROWS, 1)
    flags = jnp.broadcast_to(receivers[0][:, None], (2 * GROUP, HD))
    dma = pltpu.SemaphoreType.DMA
    vmem = pl.BlockSpec(memory_space=pltpu.VMEM)
    hbm = pl.BlockSpec(memory_space=pl.ANY)
    attended = pl.pallas_call(
        kernel,
        out_shape=jax.ShapeDtypeStruct((ROWS, 2 * GROUP * HD), BF),
        in_specs=[vmem] * 7 + [hbm] * 4,
        out_specs=vmem,
        scratch_shapes=[
            pltpu.VMEM((EX, 32, 2 * HD), BF),
            pltpu.VMEM((EX, 32, 2 * HD), BF),
            pltpu.VMEM((EX, 32, 2 * HD), BF),
            pltpu.VMEM((EX, EX, 32, 2 * HD), BF),
            pltpu.VMEM((EX, 64, SEC * ROWS), BF),
            pltpu.VMEM((2, EX, HALF, 2 * HD), BF),
            pltpu.VMEM((HALF, ROWS), F32),
            pltpu.VMEM((2, SEC, TP, HALF, HD), BF),
            pltpu.VMEM((2, EX, HALF, HD), BF),
            pltpu.VMEM((ROWS, SEC * ROWS), BF),
            pltpu.VMEM((2, TP, HALF, 2 * HD), BF),
            pltpu.VMEM((2, TP, HALF, 2 * HD), BF),
            pltpu.VMEM((2, 8, HALF), F32),
            pltpu.VMEM((2, TP, 8, HALF), F32),
            pltpu.VMEM((ROWS, 2 * HD), BF),
            pltpu.VMEM((2 * GROUP, ROWS, ROWS), BF),
            pltpu.VMEM((ROWS, SEC * ROWS), BF),
            pltpu.VMEM((ROWS, 2 * HD), BF),
            pltpu.VMEM((ROWS, 2 * GROUP * HD), BF),
            pltpu.VMEM((ROWS, 2 * HD), BF),
            dma((4,)),
            dma((EX,)),
            dma((EX,)),
            dma((EX,)),
            dma((EX,)),
            dma((EX,)),
            dma((EX,)),
            dma((2, 4)),
            dma((2, 4)),
            dma((2, 3)),
            dma((2, 3)),
            dma((2, 8)),
            dma((2, 8)),
            dma((2, EX - 1)),
            dma((2, EX)),
            dma((2, EX)),
            dma((2, EX)),
            dma((2, TP)),
            dma((2, TP)),
            dma((2, TP)),
            dma((2, TP)),
        ],
        compiler_params=pltpu.CompilerParams(
            collective_id=0, has_side_effects=True, vmem_limit_bytes=56 * 2**20
        ),
    )(
        corrupt,
        clean,
        target,
        weight,
        value_weight[0].T,
        flags,
        norm_gain,
        residual[0, 0],
        clean_values[0, 0],
        queries[0, 0],
        key_vectors[0, 0],
    )
    return attended.reshape(1, 1, ROWS, -1)


def solution(mesh):
    return jax.shard_map(
        per_device,
        mesh=mesh,
        in_specs=(
            P("section", "ex", None, "tp"),
            P("section", "ex", None, "tp"),
            P("ex", None),
            P("section", "tp"),
            P("section", "tp", "ex"),
            P("section", "ex", None, "tp"),
            P("section", "tp"),
            P("section", "tp", "ex"),
            P("section", "ex", None, "tp"),
            P("section", "ex", None, "tp"),
            P("section", "ex", None, "tp"),
            P("section", "tp"),
        ),
        out_specs=P("section", "ex", None, "tp"),
        check_vma=False,
    )
```

time: 303 us -> 123 us (0.41); the launches traced: 300 us -> 123 us
  waiting for transfers between devices: 181 us -> 0 us
  Pallas kernels: 0 us -> 110 us
  starting transfers between devices: 34.7 us -> 0 us
  matrix products: 23.3 us -> 0 us
  local copies, waits for them, and re-layouts: 31.3 us -> 8.99 us
  between operations: 14.7 us -> 1.3 us
  other arithmetic: 14.9 us -> 2.84 us
    all_gather x5 -> x0, waiting for transfers between devices: 132 us -> none  [the longest x1 59.7 us: per_device(): differences = lax.all_gather(difference, ('section', 'tp'))]
    pallas_call x0 -> x1, Pallas kernels: none -> 110 us  [per_device(): pl.pallas_call(kernel, out_shape=jax.ShapeDtypeStruct((ROWS, 2 * GROUP *...]
    all_to_all x5 -> x0, waiting for transfers between devices: 34.9 us -> none  [the longest x1 13.7 us: per_device(): lax.all_to_all(corrupt[None], 'ex', split_axis=1, concat_axis=0, tiled=True)]
    all_to_all x5 -> x0, starting transfers between devices: 24.9 us -> none  [the longest x1 8.66 us: per_device(): lax.all_to_all(corrupt[None], 'ex', split_axis=1, concat_axis=0, tiled=True)]
    dot_general x5 -> x0, matrix products: 23.3 us -> none  [the longest x1 6.55 us: per_device(): jnp.einsum('spc,nsc->pn', scaled, value_columns.reshape(-1, sections, wid...]
    ppermute x1 -> x0, waiting for transfers between devices: 13 us -> none  [per_device(): lax.ppermute(rows, ('section', 'ex', 'tp'), chunk_moves(sections, everyon...]
    ppermute x1 -> x0, starting transfers between devices: 9.66 us -> none  [per_device(): lax.ppermute(rows, ('section', 'ex', 'tp'), chunk_moves(sections, everyon...]
    reduce_sum x4 -> x0, other arithmetic: 8.72 us -> none  [the longest x1 5.11 us: attend(): jnp.sum(exponent, axis=-1, keepdims=True)]
  transfers between devices with their start and end apart: 11 -> 0, of which waited for: 8 -> 0; matrix products, arithmetic and copies ran while one was open for 18% -> 0% of each run, Pallas kernels for 0% -> 0%
where the time goes in v2:
time: 123 us
  Pallas kernels  110 us (89%)
  local copies, waits for them, and re-layouts  8.99 us (7%)
  other arithmetic  2.84 us (2%)
  between operations  1.3 us (1%)
    pallas_call x1, Pallas kernels, per_device(): pl.pallas_call(kernel, out_shape=jax.ShapeDtypeStruct((ROWS, 2 * GROUP *...  110 us

profile of v2, /device:TPU:7, one launch (start us, length us, event | category | flops | bytes accessed | tf_op | source)
XLA Modules:
  0.0 123.0 jit_solution(11752496334960852525)
XLA Ops:
  0.0 0.7 broadcast_subtract_fusion
  0.7 0.6 fusion
  2.5 1.3 %broadcast_in_dim.9.flags = s32[8,128]{1,0:T(8,128)} broadcast(s32[8]{0:T(128)} %bitcast.35), dimensions={0} | broadcast | bytes 4128 | tf_op jit(solution)/shard_map/broadcast_in_dim | solution.py:574
  3.9 0.7 bitcast_add_fusion
  4.6 1.0 reshape.38.target
  5.5 1.0 dynamic-slice_bitcast_fusion.1
  6.6 0.8 copy.13
  7.4 1.0 dynamic-slice_bitcast_fusion.3
  8.4 0.7 pad_maximum_fusion.1.clean
  9.1 1.0 constant_dynamic-slice_fusion.1
  10.1 0.7 pad_maximum_fusion.corrupt
  10.9 109.9 %shard_map.118 = bf16[512,1024]{1,0:T(8,128)(2,1)} custom-call(bf16[16,32,256]{2,1,0:T(8,128)(2,1)} %pad_maximum_fusion.corrupt, bf16[512,256]{1,0:T(8,128)(2,1)} %pad_maximum_fusion.1.clean, s32[512,1]{1,0:T(8,128)} %reshape.38.target, bf16[16,32,256]{2,1,0:T(8,128)(2,1)} %bitcast.29, bf16[64,2048]{1,0:T(8,128)(2,1)} %bitcast.32, ...), custom_call_target="tpu_custom_call" | custom-call | tf_op jit(solution)/shard_map/pallas_call | solution.py:578
  120.8 2.3 %copy.16 = bf16[1,1,512,1024]{3,2,1,0:T(8,128)(2,1)} copy(bf16[1,1,512,1024]{3,2,1,0:T(8,128)(2,1)} %bitcast.26) | data formatting | bytes 2097152
  (1 shorter events, 0.0 us)

commit v3 on v2

--- a/solution.py
+++ b/solution.py
@@ -37,13 +37,14 @@
 
 
 def kernel(
-    corrupt,
-    clean,
-    target,
-    weight,
-    value_weight,
-    flags,
+    senders,
+    receivers,
+    donors,
     gain,
+    corrupt_hbm,
+    clean_hbm,
+    weight_hbm,
+    value_weight_hbm,
     residual_hbm,
     clean_values_hbm,
     queries_hbm,
@@ -69,6 +70,13 @@
     clean_values,
     queries,
     keys,
+    corrupt_all,
+    clean_all,
+    weight_all,
+    corrupt,
+    clean,
+    weight,
+    flags,
     local_sem,
     patch_send,
     patch_recv,
@@ -104,8 +112,14 @@
         pltpu.make_async_copy(keys_hbm, keys, local_sem.at[1]),
         pltpu.make_async_copy(residual_hbm, residual, local_sem.at[2]),
         pltpu.make_async_copy(clean_values_hbm, clean_values, local_sem.at[3]),
+        pltpu.make_async_copy(clean_hbm, clean_all, local_sem.at[4]),
     ]
-    for load in loads:
+    first_loads = [
+        pltpu.make_async_copy(corrupt_hbm, corrupt_all, local_sem.at[5]),
+        pltpu.make_async_copy(weight_hbm, weight_all, local_sem.at[6]),
+        pltpu.make_async_copy(value_weight_hbm, value_weights.at[ex], local_sem.at[7]),
+    ]
+    for load in first_loads:
         load.start()
 
     barrier = pltpu.get_barrier_semaphore()
@@ -127,6 +141,21 @@
             barrier, inc=1, device_id={"section": s, "tp": t}, device_id_type=MESH
         )
 
+    heads_here = 2 * GROUP
+    feature = lax.broadcasted_iota(jnp.int32, (heads_here * HD, HD), 0)
+    lane = lax.broadcasted_iota(jnp.int32, (heads_here * HD, HD), 1)
+    picks = []
+    for i in (0, 1):
+        head = senders[:, i : i + 1] - heads_here * tp
+        picks.append((feature - lane == head * HD).astype(F32).astype(BF))
+    pick = jnp.concatenate(picks, axis=1)
+    first_loads[0].wait()
+    corrupt[...] = (
+        jnp.dot(corrupt_all[...], pick, preferred_element_type=F32)
+        .astype(BF)
+        .reshape(EX, ROWS // EX, 2 * HD)
+    )
+
     pl.semaphore_wait(barrier, 2 * (EX - 1))
 
     @pl.loop(1, EX)
@@ -135,6 +164,16 @@
         remote(
             corrupt.at[other], arrived.at[ex], patch_send.at[i], patch_recv.at[ex], {"ex": other}
         ).start()
+
+    arrived[ex] = corrupt[ex]
+    first_loads[1].wait()
+    weight[...] = (
+        lax.dot_general(
+            weight_all[...], pick, (((0,), (0,)), ((), ())), preferred_element_type=F32
+        )
+        .astype(BF)
+        .reshape(EX, ROWS // EX, 2 * HD)
+    )
 
     @pl.loop(1, EX)
     def _(i):
@@ -147,9 +186,10 @@
             {"section": s, "tp": t},
         ).start()
 
-    arrived[ex] = corrupt[ex]
     weights[ex, mine] = weight[group]
-    value_weights[ex] = value_weight[...]
+    for load in loads:
+        load.start()
+    first_loads[2].wait()
 
     def ring_start(which, buffer):
         block = buffer.at[ex]
@@ -244,6 +284,26 @@
     loads[1].wait()
     weigh_heads(0, 1)
 
+    block = ROWS // EX
+    same = lax.broadcasted_iota(jnp.int32, (block, block), 0) == lax.broadcasted_iota(
+        jnp.int32, (block, block), 1
+    )
+    donor = dot_nt(same.astype(F32).astype(BF), donors[...].astype(F32).astype(BF))
+    row = lax.broadcasted_iota(jnp.int32, (block, ROWS), 0)
+    column = lax.broadcasted_iota(jnp.int32, (block, ROWS), 1)
+    offset = (column - row).astype(F32)
+    onehot = jnp.concatenate(
+        [
+            (offset == donor[:, e : e + 1] * block).astype(F32).astype(BF)
+            for e in range(EX)
+        ],
+        axis=0,
+    )
+    loads[4].wait()
+    clean[...] = jnp.dot(clean_all[...], pick, preferred_element_type=F32).astype(BF)
+    for h in range(heads_here):
+        flags[h : h + 1, :] = jnp.broadcast_to(receivers[:, h : h + 1], (1, HD))
+
     @pl.loop(1, EX)
     def _(i):
         other = lax.rem(mine + i, EX)
@@ -264,8 +324,6 @@
             arrived.at[other], arrived.at[other], patch_send.at[i], patch_recv.at[other], {"ex": other}
         ).wait_recv()
 
-    column = lax.broadcasted_iota(jnp.int32, (ROWS, ROWS), 1)
-    onehot = (column == target[...]).astype(F32).astype(BF)
     moved = jnp.dot(
         onehot, arrived[...].reshape(ROWS, 2 * HD), preferred_element_type=F32
     ).astype(BF)
@@ -540,16 +598,6 @@
             ).wait_send()
 
 
-def pick_columns(array, ids):
-    parts = [lax.dynamic_slice_in_dim(array, ids[i] * HD, HD, 1) for i in range(ids.shape[0])]
-    return jnp.concatenate(parts, axis=1)
-
-
-def pick_rows(array, ids):
-    parts = [lax.dynamic_slice_in_dim(array, ids[i] * HD, HD, 0) for i in range(ids.shape[0])]
-    return jnp.concatenate(parts, axis=0)
-
-
 def per_device(
     clean_heads,
     corrupt_heads,
@@ -564,21 +612,13 @@
     key_vectors,
     receivers,
 ):
-    heads_here = clean_heads.shape[3] // HD
-    ids = senders[0] - lax.axis_index("tp") * heads_here
-    corrupt = pick_columns(corrupt_heads[0, 0], ids).reshape(EX, ROWS // EX, 2 * HD)
-    clean = pick_columns(clean_heads[0, 0], ids)
-    weight = pick_rows(out_weight[0], ids).T.reshape(EX, ROWS // EX, 2 * HD)
-    block = ROWS // EX
-    target = (donors.T * block + jnp.arange(block, dtype=jnp.int32)[None, :]).reshape(ROWS, 1)
-    flags = jnp.broadcast_to(receivers[0][:, None], (2 * GROUP, HD))
     dma = pltpu.SemaphoreType.DMA
     vmem = pl.BlockSpec(memory_space=pltpu.VMEM)
     hbm = pl.BlockSpec(memory_space=pl.ANY)
     attended = pl.pallas_call(
         kernel,
         out_shape=jax.ShapeDtypeStruct((ROWS, 2 * GROUP * HD), BF),
-        in_specs=[vmem] * 7 + [hbm] * 4,
+        in_specs=[vmem] * 4 + [hbm] * 8,
         out_specs=vmem,
         scratch_shapes=[
             pltpu.VMEM((EX, 32, 2 * HD), BF),
@@ -601,7 +641,14 @@
             pltpu.VMEM((ROWS, 2 * HD), BF),
             pltpu.VMEM((ROWS, 2 * GROUP * HD), BF),
             pltpu.VMEM((ROWS, 2 * HD), BF),
-            dma((4,)),
+            pltpu.VMEM((ROWS, 8 * HD), BF),
+            pltpu.VMEM((ROWS, 8 * HD), BF),
+            pltpu.VMEM((8 * HD, ROWS), BF),
+            pltpu.VMEM((EX, 32, 2 * HD), BF),
+            pltpu.VMEM((ROWS, 2 * HD), BF),
+            pltpu.VMEM((EX, 32, 2 * HD), BF),
+            pltpu.VMEM((2 * GROUP, HD), jnp.int32),
+            dma((8,)),
             dma((EX,)),
             dma((EX,)),
             dma((EX,)),
@@ -627,13 +674,14 @@
             collective_id=0, has_side_effects=True, vmem_limit_bytes=56 * 2**20
         ),
     )(
-        corrupt,
-        clean,
-        target,
-        weight,
+        senders,
+        receivers,
+        donors.T,
+        norm_gain,
+        corrupt_heads[0, 0],
+        clean_heads[0, 0],
+        out_weight[0],
         value_weight[0].T,
-        flags,
-        norm_gain,
         residual[0, 0],
         clean_values[0, 0],
         queries[0, 0],

time: 123 us -> 113 us (0.919)
  local copies, waits for them, and re-layouts: 8.99 us -> 2.26 us
  other arithmetic: 2.84 us -> 0 us
  between operations: 1.3 us -> 0.01 us
    dynamic_slice x3 -> x0, local copies, waits for them, and re-layouts: 2.96 us -> none  [the longest x2 1.98 us: pick_columns(): lax.dynamic_slice_in_dim(array, ids[i] * HD, HD, 1)]
    concatenate x2 -> x0, other arithmetic: 1.47 us -> none  [pick_columns(): return jnp.concatenate(parts, axis=1)]
    broadcast_in_dim x1 -> x0, local copies, waits for them, and re-layouts: 1.32 us -> none  [per_device(): flags = jnp.broadcast_to(receivers[0][:, None], (2 * GROUP, HD))]
where the time goes in v3:
time: 113 us
  Pallas kernels  110 us (97%)
  local copies, waits for them, and re-layouts  2.26 us (2%)
    pallas_call x1, Pallas kernels, per_device(): pl.pallas_call(kernel, out_shape=jax.ShapeDtypeStruct((ROWS, 2 * GROUP *...  110 us
    unnamed x1, local copies, waits for them, and re-layouts  2.26 us

profile of v3, /device:TPU:7, one launch (start us, length us, event | category | flops | bytes accessed | tf_op | source)
XLA Modules:
  0.0 112.5 jit_solution(8765757882666358436)
XLA Ops:
  0.0 110.3 %shard_map.118 = bf16[512,1024]{1,0:T(8,128)(2,1)} custom-call(s32[1,2]{1,0:T(1,128)} %senders.1, s32[1,8]{1,0:T(1,128)} %receivers.1, s32[16,32]{1,0:T(8,128)} %bitcast.21, bf16[1,2048]{1,0:T(2,128)(2,1)} %gain.1, bf16[512,1024]{1,0:T(8,128)(2,1)} %bitcast.14, bf16[512,1024]{1,0:T(8,128)(2,1)} %bitcast.15, bf16[1024,512]{1,0:T(8,128)(2,1)} %bitcast.16, ...), custom_call_target="tpu_custom_call" | custom-call | tf_op jit(solution)/shard_map/pallas_call | solution.py:618
  110.3 2.3 %copy.14 = bf16[1,1,512,1024]{3,2,1,0:T(8,128)(2,1)} copy(bf16[1,1,512,1024]{3,2,1,0:T(8,128)(2,1)} %bitcast.12) | data formatting | bytes 2097152

commit v4 on v3

--- a/solution.py
+++ b/solution.py
@@ -191,51 +191,50 @@
         load.start()
     first_loads[2].wait()
 
+    ring_up = 2 * lax.rem(chip + 1, CHIPS) + core
+    ring_down = 2 * lax.rem(chip + CHIPS - 1, CHIPS) + core
+    ring_side = 2 * chip + 1 - core
+
+    def ring_copy(which, buffer, upward, origin, part, step):
+        middle = buffer.shape[1] // 2
+        ref = buffer.at[origin, pl.ds(part * middle, middle)]
+        send, recv = (up_send, up_recv) if upward else (down_send, down_recv)
+        index = 2 * step + part
+        return remote(
+            ref,
+            ref,
+            send.at[which, index],
+            recv.at[which, index],
+            {"ex": ring_up if upward else ring_down},
+        )
+
+    def to_side(which, buffer, origin, slot):
+        ref = buffer.at[origin]
+        remote(
+            ref, ref, side_send.at[which, slot], side_recv.at[which, slot], {"ex": ring_side}
+        ).start()
+
     def ring_start(which, buffer):
-        block = buffer.at[ex]
-        up = 2 * lax.rem(chip + 1, CHIPS) + core
-        down = 2 * lax.rem(chip + CHIPS - 1, CHIPS) + core
-        remote(block, block, up_send.at[which, 0], up_recv.at[which, 0], {"ex": up}).start()
-        remote(block, block, down_send.at[which, 0], down_recv.at[which, 0], {"ex": down}).start()
-        remote(
-            block, block, side_send.at[which, 0], side_recv.at[which, 0], {"ex": 2 * chip + 1 - core}
-        ).start()
+        for part in (0, 1):
+            ring_copy(which, buffer, True, ex, part, 0).start()
+            ring_copy(which, buffer, False, ex, part, 0).start()
+        to_side(which, buffer, ex, 0)
 
     def ring_relay(which, buffer, step):
-        up = 2 * lax.rem(chip + 1, CHIPS) + core
-        down = 2 * lax.rem(chip + CHIPS - 1, CHIPS) + core
-        side = 2 * chip + 1 - core
-        block = buffer.at[2 * lax.rem(chip + CHIPS - step, CHIPS) + core]
-        remote(
-            block, block, up_send.at[which, step - 1], up_recv.at[which, step - 1], {"ex": up}
-        ).wait_recv()
+        above = 2 * lax.rem(chip + CHIPS - step, CHIPS) + core
+        below = 2 * lax.rem(chip + step, CHIPS) + core
+        for part in (0, 1):
+            if step < 4 or part == 0:
+                ring_copy(which, buffer, True, above, part, step - 1).wait_recv()
+            if step < 3 or (step == 3 and part == 0):
+                ring_copy(which, buffer, True, above, part, step).start()
+            if step < 4 or part == 1:
+                ring_copy(which, buffer, False, below, part, step - 1).wait_recv()
+            if step < 3 or (step == 3 and part == 1):
+                ring_copy(which, buffer, False, below, part, step).start()
+        to_side(which, buffer, above, step)
         if step < 4:
-            remote(
-                block, block, up_send.at[which, step], up_recv.at[which, step], {"ex": up}
-            ).start()
-        remote(
-            block, block, side_send.at[which, step], side_recv.at[which, step], {"ex": side}
-        ).start()
-        if step < 4:
-            block = buffer.at[2 * lax.rem(chip + step, CHIPS) + core]
-            remote(
-                block,
-                block,
-                down_send.at[which, step - 1],
-                down_recv.at[which, step - 1],
-                {"ex": down},
-            ).wait_recv()
-            if step < 3:
-                remote(
-                    block, block, down_send.at[which, step], down_recv.at[which, step], {"ex": down}
-                ).start()
-            remote(
-                block,
-                block,
-                side_send.at[which, 4 + step],
-                side_recv.at[which, 4 + step],
-                {"ex": side},
-            ).start()
+            to_side(which, buffer, below, 4 + step)
 
     def ring_finish(which, buffer):
         side = 2 * chip + 1 - core
@@ -247,18 +246,16 @@
             ).wait_recv()
 
     def ring_drain(which, buffer):
+        for step in range(4):
+            for part in (0, 1):
+                if step < 3 or part == 0:
+                    ring_copy(which, buffer, True, ex, part, step).wait_send()
+                if step < 3 or part == 1:
+                    ring_copy(which, buffer, False, ex, part, step).wait_send()
         block = buffer.at[ex]
-        for step in range(4):
-            remote(
-                block, block, up_send.at[which, step], up_recv.at[which, step], {"ex": 0}
-            ).wait_send()
-        for step in range(3):
-            remote(
-                block, block, down_send.at[which, step], down_recv.at[which, step], {"ex": 0}
-            ).wait_send()
-        for step in range(8):
-            remote(
-                block, block, side_send.at[which, step], side_recv.at[which, step], {"ex": 0}
+        for slot in range(8):
+            remote(
+                block, block, side_send.at[which, slot], side_recv.at[which, slot], {"ex": ring_side}
             ).wait_send()
 
     def softmax(scores):
@@ -279,10 +276,6 @@
                 column = lax.broadcasted_iota(jnp.int32, scores.shape, 1)
                 scores = jnp.where(row >= column, scores, -jnp.inf)
                 probabilities[h, half * HALF : (half + 1) * HALF, :length] = softmax(scores)
-
-    loads[0].wait()
-    loads[1].wait()
-    weigh_heads(0, 1)
 
     block = ROWS // EX
     same = lax.broadcasted_iota(jnp.int32, (block, block), 0) == lax.broadcasted_iota(
@@ -299,10 +292,27 @@
         ],
         axis=0,
     )
-    loads[4].wait()
-    clean[...] = jnp.dot(clean_all[...], pick, preferred_element_type=F32).astype(BF)
-    for h in range(heads_here):
-        flags[h : h + 1, :] = jnp.broadcast_to(receivers[:, h : h + 1], (1, HD))
+
+    @pl.loop(1, EX)
+    def _(i):
+        other = lax.rem(ex + i, EX)
+        remote(
+            arrived.at[other], arrived.at[other], patch_send.at[i], patch_recv.at[other], {"ex": other}
+        ).wait_recv()
+
+    moved = jnp.dot(
+        onehot, arrived[...].reshape(ROWS, 2 * HD), preferred_element_type=F32
+    ).astype(BF)
+    patched[...] = moved.reshape(EX, ROWS // EX, 2 * HD)
+
+    @pl.loop(1, EX)
+    def _(i):
+        other = lax.rem(ex + i, EX)
+        remote(
+            patched.at[other], returned.at[ex], back_send.at[i], back_recv.at[ex], {"ex": other}
+        ).start()
+
+    returned[ex] = patched[ex]
 
     @pl.loop(1, EX)
     def _(i):
@@ -316,28 +326,13 @@
         ).wait_recv()
 
     ring_start(0, weights)
-
-    @pl.loop(1, EX)
-    def _(i):
-        other = lax.rem(ex + i, EX)
-        remote(
-            arrived.at[other], arrived.at[other], patch_send.at[i], patch_recv.at[other], {"ex": other}
-        ).wait_recv()
-
-    moved = jnp.dot(
-        onehot, arrived[...].reshape(ROWS, 2 * HD), preferred_element_type=F32
-    ).astype(BF)
-    patched[...] = moved.reshape(EX, ROWS // EX, 2 * HD)
-
-    @pl.loop(1, EX)
-    def _(i):
-        other = lax.rem(ex + i, EX)
-        remote(
-            patched.at[other], returned.at[ex], back_send.at[i], back_recv.at[ex], {"ex": other}
-        ).start()
-
-    returned[ex] = patched[ex]
-    weigh_heads(1, 3)
+    loads[4].wait()
+    clean[...] = jnp.dot(clean_all[...], pick, preferred_element_type=F32).astype(BF)
+    for h in range(heads_here):
+        flags[h : h + 1, :] = jnp.broadcast_to(receivers[:, h : h + 1], (1, HD))
+    loads[0].wait()
+    loads[1].wait()
+    weigh_heads(0, 2)
 
     @pl.loop(1, EX)
     def _(i):
@@ -354,40 +349,71 @@
     differences[0, mine] = change[:HALF].astype(BF)
     differences[1, mine] = change[HALF:].astype(BF)
 
-    def along(axis, half, block, slot):
+    axes = (("tp", "section"), ("section", "tp"))
+    places = ((tp, sec), (sec, tp))
+
+    def block_of(half, first, second):
+        first, second = lax.rem(first + 8, 4), lax.rem(second + 8, 4)
+        return TP * second + first if half == 0 else TP * first + second
+
+    def difference_send(half, ref, block, axis, step, slot):
         here = sec if axis == "section" else tp
-        for i in range(1, 4):
-            ref = differences.at[half, block]
-            remote(
-                ref,
-                ref,
-                diff_send.at[half, slot + i - 1],
-                diff_recv.at[half, block],
-                {axis: lax.rem(here + i, 4)},
-            ).start()
+        remote(
+            ref,
+            ref,
+            diff_send.at[half, slot],
+            diff_recv.at[half, block],
+            {axis: lax.rem(here + step + 4, 4)},
+        ).start()
+
+    def to_neighbours(half, phase, block, slot):
+        ref = differences.at[half, block]
+        difference_send(half, ref, block, axes[half][phase], 1, slot)
+        difference_send(half, ref, block, axes[half][phase], -1, slot + 1)
+
+    def pass_on(half, phase, block, step, slot):
+        part = pl.ds(0, HALF // 2) if step > 0 else pl.ds(HALF // 2, HALF // 2)
+        ref = differences.at[half, block, part]
+        difference_send(half, ref, block, axes[half][phase], step, slot)
 
     def difference_wait(half, block):
         ref = differences.at[half, block]
         remote(ref, ref, diff_send.at[half, 0], diff_recv.at[half, block], {"ex": ex}).wait_recv()
 
-    along("tp", 0, mine, 0)
-    along("section", 1, mine, 0)
-    along("section", 0, mine, 3)
-    along("tp", 1, mine, 3)
+    def second_phase(k):
+        shift = (0, -1, 1, 2)[k]
+        for half in (0, 1):
+            first, second = places[half]
+            for step in (1, -1):
+                block = block_of(half, first + shift, second - step)
+                difference_wait(half, block)
+                pass_on(half, 1, block, step, 12 + 2 * k + (step < 0))
+
+    for half in (0, 1):
+        to_neighbours(half, 0, mine, 0)
+    for half in (0, 1):
+        to_neighbours(half, 1, mine, 2)
+    for half in (0, 1):
+        first, second = places[half]
+        for step in (1, -1):
+            block = block_of(half, first - step, second)
+            difference_wait(half, block)
+            pass_on(half, 0, block, step, 10 + (step < 0))
+            to_neighbours(half, 1, block, 4 if step > 0 else 6)
     ring_relay(0, weights, 1)
-    for i in range(1, 4):
-        block = TP * sec + lax.rem(tp + i, TP)
-        difference_wait(0, block)
-        along("section", 0, block, 3 + 3 * i)
-        block = TP * lax.rem(sec + i, SEC) + tp
-        difference_wait(1, block)
-        along("tp", 1, block, 3 + 3 * i)
+    second_phase(0)
     ring_relay(0, weights, 2)
-    weigh_heads(3, 5)
+    for half in (0, 1):
+        first, second = places[half]
+        block = block_of(half, first + 2, second)
+        difference_wait(half, block)
+        to_neighbours(half, 1, block, 8)
+    second_phase(1)
     ring_relay(0, weights, 3)
+    second_phase(2)
+    ring_relay(0, weights, 4)
     ring_start(1, value_weights)
-    weigh_heads(5, 7)
-    ring_relay(0, weights, 4)
+    second_phase(3)
     ring_finish(0, weights)
 
     def carry(half):
@@ -395,8 +421,9 @@
         def _(r):
             for t in range(TP):
                 block = TP * r + t
-                first = (block // TP == sec) if half == 0 else (t == tp)
-                @pl.when(jnp.logical_not(first))
+                opposite = lax.rem(sec + 2, SEC) if half == 0 else lax.rem(tp + 2, TP)
+
+                @pl.when((r if half == 0 else t) == opposite)
                 def _():
                     difference_wait(half, block)
 
@@ -437,8 +464,9 @@
     ring_relay(1, value_weights, 1)
     carry(1)
     ring_relay(1, value_weights, 2)
-    weigh_heads(7, 8)
+    weigh_heads(2, 5)
     ring_relay(1, value_weights, 3)
+    weigh_heads(5, 8)
     ring_relay(1, value_weights, 4)
     ring_finish(1, value_weights)
     loads[2].wait()
@@ -564,10 +592,14 @@
     ring_drain(1, value_weights)
     for half in (0, 1):
 
-        @pl.loop(0, EX - 1)
+        @pl.loop(0, 10)
         def _(i):
             ref = differences.at[half, 0]
             remote(ref, ref, diff_send.at[half, i], diff_recv.at[half, 0], {"ex": 0}).wait_send()
+            ref = differences.at[half, 0, pl.ds(0, HALF // 2)]
+            remote(
+                ref, ref, diff_send.at[half, 10 + i], diff_recv.at[half, 0], {"ex": 0}
+            ).wait_send()
 
         @pl.loop(1, EX)
         def _(i):
@@ -655,13 +687,13 @@
             dma((EX,)),
             dma((EX,)),
             dma((EX,)),
-            dma((2, 4)),
-            dma((2, 4)),
-            dma((2, 3)),
-            dma((2, 3)),
             dma((2, 8)),
             dma((2, 8)),
-            dma((2, EX - 1)),
+            dma((2, 8)),
+            dma((2, 8)),
+            dma((2, 8)),
+            dma((2, 8)),
+            dma((2, 20)),
             dma((2, EX)),
             dma((2, EX)),
             dma((2, EX)),

time: 113 us -> 106 us (0.938)
  the two profiles are of different devices: /device:TPU:7 before, /device:TPU:49 now
where the time goes in v4:
time: 106 us
  Pallas kernels  104 us (98%)
  local copies, waits for them, and re-layouts  2.26 us (2%)
    pallas_call x1, Pallas kernels, per_device(): pl.pallas_call(kernel, out_shape=jax.ShapeDtypeStruct((ROWS, 2 * GROUP *...  104 us
    unnamed x1, local copies, waits for them, and re-layouts  2.26 us

profile of v4, /device:TPU:49, one launch (start us, length us, event | category | flops | bytes accessed | tf_op | source)
XLA Modules:
  0.0 106.3 jit_solution(15616687387342552260)
XLA Ops:
  0.0 104.0 %shard_map.118 = bf16[512,1024]{1,0:T(8,128)(2,1)} custom-call(s32[1,2]{1,0:T(1,128)} %senders.1, s32[1,8]{1,0:T(1,128)} %receivers.1, s32[16,32]{1,0:T(8,128)} %bitcast.21, bf16[1,2048]{1,0:T(2,128)(2,1)} %gain.1, bf16[512,1024]{1,0:T(8,128)(2,1)} %bitcast.14, bf16[512,1024]{1,0:T(8,128)(2,1)} %bitcast.15, bf16[1024,512]{1,0:T(8,128)(2,1)} %bitcast.16, ...), custom_call_target="tpu_custom_call" | custom-call | tf_op jit(solution)/shard_map/pallas_call | solution.py:650
  104.1 2.3 %copy.14 = bf16[1,1,512,1024]{3,2,1,0:T(8,128)(2,1)} copy(bf16[1,1,512,1024]{3,2,1,0:T(8,128)(2,1)} %bitcast.12) | data formatting | bytes 2097152

commit v5 on v4

--- a/solution.py
+++ b/solution.py
@@ -409,11 +409,11 @@
         difference_wait(half, block)
         to_neighbours(half, 1, block, 8)
     second_phase(1)
+    second_phase(2)
     ring_relay(0, weights, 3)
-    second_phase(2)
+    second_phase(3)
     ring_relay(0, weights, 4)
     ring_start(1, value_weights)
-    second_phase(3)
     ring_finish(0, weights)
 
     def carry(half):
@@ -464,10 +464,31 @@
     ring_relay(1, value_weights, 1)
     carry(1)
     ring_relay(1, value_weights, 2)
-    weigh_heads(2, 5)
+    weigh_heads(2, 4)
     ring_relay(1, value_weights, 3)
-    weigh_heads(5, 8)
+    weigh_heads(4, 6)
     ring_relay(1, value_weights, 4)
+    @pl.loop(1, EX)
+    def _(i):
+        remote(corrupt.at[0], arrived.at[0], patch_send.at[i], patch_recv.at[0], {"ex": 0}).wait_send()
+        remote(patched.at[0], returned.at[0], back_send.at[i], back_recv.at[0], {"ex": 0}).wait_send()
+        remote(
+            weight.at[0], weights.at[0, 0], piece_send.at[i], piece_recv.at[0], {"ex": 0}
+        ).wait_send()
+
+    ring_drain(0, weights)
+    for half in (0, 1):
+
+        @pl.loop(0, 10)
+        def _(i):
+            ref = differences.at[half, 0]
+            remote(ref, ref, diff_send.at[half, i], diff_recv.at[half, 0], {"ex": 0}).wait_send()
+            ref = differences.at[half, 0, pl.ds(0, HALF // 2)]
+            remote(
+                ref, ref, diff_send.at[half, 10 + i], diff_recv.at[half, 0], {"ex": 0}
+            ).wait_send()
+
+    weigh_heads(6, 8)
     ring_finish(1, value_weights)
     loads[2].wait()
     loads[3].wait()
@@ -577,29 +598,8 @@
 
     finish_stream(0)
     finish_stream(1)
-    attend(0)
-    attend(1)
-
-    @pl.loop(1, EX)
-    def _(i):
-        remote(corrupt.at[0], arrived.at[0], patch_send.at[i], patch_recv.at[0], {"ex": 0}).wait_send()
-        remote(patched.at[0], returned.at[0], back_send.at[i], back_recv.at[0], {"ex": 0}).wait_send()
-        remote(
-            weight.at[0], weights.at[0, 0], piece_send.at[i], piece_recv.at[0], {"ex": 0}
-        ).wait_send()
-
-    ring_drain(0, weights)
     ring_drain(1, value_weights)
     for half in (0, 1):
-
-        @pl.loop(0, 10)
-        def _(i):
-            ref = differences.at[half, 0]
-            remote(ref, ref, diff_send.at[half, i], diff_recv.at[half, 0], {"ex": 0}).wait_send()
-            ref = differences.at[half, 0, pl.ds(0, HALF // 2)]
-            remote(
-                ref, ref, diff_send.at[half, 10 + i], diff_recv.at[half, 0], {"ex": 0}
-            ).wait_send()
 
         @pl.loop(1, EX)
         def _(i):
@@ -612,6 +612,10 @@
                 {"ex": 0},
             ).wait_send()
 
+    attend(0)
+    attend(1)
+
+    for half in (0, 1):
         for i in range(1, TP):
             other = lax.rem(tp + i, TP)
             remote(

time: 106 us -> 105 us (level)
  the two profiles are of different devices: /device:TPU:49 before, /device:TPU:7 now
where the time goes in v5:
time: 105 us; the launch traced here: 104 us
  Pallas kernels  102 us (97%)
  local copies, waits for them, and re-layouts  2.26 us (2%)
    pallas_call x1, Pallas kernels, per_device(): pl.pallas_call(kernel, out_shape=jax.ShapeDtypeStruct((ROWS, 2 * GROUP *...  102 us
    unnamed x1, local copies, waits for them, and re-layouts  2.26 us

profile of v5, /device:TPU:7, one launch (start us, length us, event | category | flops | bytes accessed | tf_op | source)
XLA Modules:
  0.0 103.9 jit_solution(11240022295313030706)
XLA Ops:
  0.0 101.6 %shard_map.118 = bf16[512,1024]{1,0:T(8,128)(2,1)} custom-call(s32[1,2]{1,0:T(1,128)} %senders.1, s32[1,8]{1,0:T(1,128)} %receivers.1, s32[16,32]{1,0:T(8,128)} %bitcast.21, bf16[1,2048]{1,0:T(2,128)(2,1)} %gain.1, bf16[512,1024]{1,0:T(8,128)(2,1)} %bitcast.14, bf16[512,1024]{1,0:T(8,128)(2,1)} %bitcast.15, bf16[1024,512]{1,0:T(8,128)(2,1)} %bitcast.16, ...), custom_call_target="tpu_custom_call" | custom-call | tf_op jit(solution)/shard_map/pallas_call | solution.py:654
  101.6 2.3 %copy.14 = bf16[1,1,512,1024]{3,2,1,0:T(8,128)(2,1)} copy(bf16[1,1,512,1024]{3,2,1,0:T(8,128)(2,1)} %bitcast.12) | data formatting | bytes 2097152

commit v6 on v5

--- a/solution.py
+++ b/solution.py
@@ -444,20 +444,22 @@
             rounded = total[...].astype(BF)
             for t in range(TP):
                 carried_out[half, r, t] = rounded[:, t * HD : (t + 1) * HD]
-                here = jnp.logical_and(r == sec, t == tp)
+            for i in range(TP):
+                owner = lax.rem(tp + i, TP)
+                here = jnp.logical_and(r == sec, owner == tp)
 
                 @pl.when(here)
                 def _():
-                    carried_in[half, group] = carried_out[half, r, t]
+                    carried_in[half, group] = carried_out[half, r, owner]
 
                 @pl.when(jnp.logical_not(here))
                 def _():
                     remote(
-                        carried_out.at[half, r, t],
+                        carried_out.at[half, r, owner],
                         carried_in.at[half, group],
-                        carry_send.at[half, TP * r + t],
+                        carry_send.at[half, TP * r + owner],
                         carry_recv.at[half, group],
-                        {"section": r, "tp": t},
+                        {"section": r, "tp": owner},
                     ).start()
 
     carry(0)

time: 105 us -> 103 us (0.981)
  Pallas kernels: 102 us -> 99.7 us
    pallas_call x1, Pallas kernels: 102 us -> 99.7 us  [per_device(): pl.pallas_call(kernel, out_shape=jax.ShapeDtypeStruct((ROWS, 2 * GROUP *...]
where the time goes in v6:
time: 103 us; the launch traced here: 102 us
  Pallas kernels  99.7 us (97%)
  local copies, waits for them, and re-layouts  2.26 us (2%)
    pallas_call x1, Pallas kernels, per_device(): pl.pallas_call(kernel, out_shape=jax.ShapeDtypeStruct((ROWS, 2 * GROUP *...  99.7 us
    unnamed x1, local copies, waits for them, and re-layouts  2.26 us

profile of v6, /device:TPU:7, one launch (start us, length us, event | category | flops | bytes accessed | tf_op | source)
XLA Modules:
  0.0 102.0 jit_solution(13001825586864780499)
XLA Ops:
  0.0 99.7 %shard_map.118 = bf16[512,1024]{1,0:T(8,128)(2,1)} custom-call(s32[1,2]{1,0:T(1,128)} %senders.1, s32[1,8]{1,0:T(1,128)} %receivers.1, s32[16,32]{1,0:T(8,128)} %bitcast.21, bf16[1,2048]{1,0:T(2,128)(2,1)} %gain.1, bf16[512,1024]{1,0:T(8,128)(2,1)} %bitcast.14, bf16[512,1024]{1,0:T(8,128)(2,1)} %bitcast.15, bf16[1024,512]{1,0:T(8,128)(2,1)} %bitcast.16, ...), custom_call_target="tpu_custom_call" | custom-call | tf_op jit(solution)/shard_map/pallas_call | solution.py:656
  99.7 2.3 %copy.14 = bf16[1,1,512,1024]{3,2,1,0:T(8,128)(2,1)} copy(bf16[1,1,512,1024]{3,2,1,0:T(8,128)(2,1)} %bitcast.12) | data formatting | bytes 2097152
